TPU v7x, 512 devices: a whole 4x4x16 slice. The times are simulated.
512 devices in a mesh: seq: 128 (over x, z, core), head: 4 (over y).
Axes of the slice: x: 4, y: 4, z: 16, core: 2. Of those that a mesh axis runs over, the one named last changes fastest.
Arguments:
- query_states: bfloat16 [16384, 2048], P('seq', 'head'), may hold values from -24.5 to 24.5
- key_states: bfloat16 [16384, 512], P('seq', 'head'), may hold values from -10.5 to 10.5
- value_states: bfloat16 [16384, 512], P('seq', 'head'), may hold values from -6 to 6
- out_weight: bfloat16 [2048, 4096], P('head'), may hold values from -0.125 to 0.125
- block_docs: int32 [128], replicated, may hold values from 0 to 63, never falling along the last dimension, each value on 1 to 32 neighbouring positions
Outputs:
- mixed: bfloat16 [16384, 4096], P('seq', 'head')
Inputs may be any that keep to these rules, and one draw needn't show every extreme that they name: `block_docs`: A document spans at most 32 blocks.
All inputs are finite; a program needn't handle non-finite values.
Results may differ from a plain program's by a relative error of at most 0.0095.
Values may be sent and summed in bfloat16 or wider, within the bound.
A program may use at most 64 MiB of HBM per device.

v0:
```python
import jax
import jax.numpy as jnp
from jax import lax
from jax.sharding import PartitionSpec as P

HD = 128
QH = 16
KH = 4
BLK = 128
DOC_BLK = 32


def passed_along(value, axis, steps):
    count = lax.axis_size(axis)
    initial, last = (max(0, -steps), min(count, count - steps))
    return lax.ppermute(value, axis, [(source, source + steps) for source in range(initial, last)])


def local(query_states, key_states, value_states, out_weight, block_docs):
    tokens_here = query_states.shape[0]
    kv_local = key_states.shape[1] // HD
    group_size = QH // KH
    block_count = block_docs.shape[0]
    blocks_here = tokens_here // BLK
    longest = min(DOC_BLK, block_count // 4)
    reach = (longest - 1 + blocks_here - 1) // blocks_here
    position = lax.axis_index("seq")
    score_scale = 1.0 / HD**0.5
    token_docs = jnp.repeat(block_docs, BLK, total_repeat_length=block_count * BLK)
    my_docs = lax.dynamic_slice_in_dim(token_docs, position * tokens_here, tokens_here, 0)
    query_blocks = query_states.reshape(tokens_here, kv_local, group_size, HD)
    query_pos = position * tokens_here + jnp.arange(tokens_here, dtype=jnp.int32)

    def absorb(state_now, offset, key_shard, value_shard):
        source = position - offset
        key_docs = lax.dynamic_slice_in_dim(
            token_docs, jnp.maximum(source, 0) * tokens_here, tokens_here, 0
        )
        key_pos = source * tokens_here + jnp.arange(tokens_here, dtype=jnp.int32)
        allowed = (
            (my_docs[:, None] == key_docs[None, :])
            & (key_pos[None, :] <= query_pos[:, None])
            & (source >= 0)
        )
        running_max, total, accumulated = state_now
        scores = (
            jnp.einsum(
                "xknv,jkv->knxj",
                query_blocks,
                key_shard.reshape(tokens_here, kv_local, HD),
                preferred_element_type=jnp.float32,
            )
            * score_scale
        )
        scores = jnp.where(allowed, scores, jnp.float32(-1e30))
        new_max = jnp.maximum(running_max, jnp.max(scores, axis=-1))
        weights = jnp.where(allowed, jnp.exp(scores - new_max[..., None]), jnp.float32(0.0))
        factor = jnp.exp(running_max - new_max)
        total = total * factor + jnp.sum(weights, axis=-1)
        product = jnp.einsum(
            "qnuh,hqm->qnum",
            weights.astype(jnp.bfloat16),
            value_shard.reshape(tokens_here, kv_local, HD),
            preferred_element_type=jnp.float32,
        )
        accumulated = accumulated * factor[..., None] + product
        return (new_max, total, accumulated)

    initial = (
        jnp.full((kv_local, group_size, tokens_here), -1e30, jnp.float32),
        jnp.zeros((kv_local, group_size, tokens_here), jnp.float32),
        jnp.zeros((kv_local, group_size, tokens_here, HD), jnp.float32),
    )
    state_now = absorb(initial, 0, key_states, value_states)
    kv_pair = jnp.stack([key_states, value_states])

    def advance(index, carried):
        current, pair_now = carried
        pair_now = passed_along(pair_now, "seq", 1)
        return (absorb(current, index + 1, pair_now[0], pair_now[1]), pair_now)

    state_now = lax.fori_loop(0, reach, advance, (state_now, kv_pair))[0]
    running_max, total, accumulated = state_now
    attended = (accumulated / total[..., None]).astype(jnp.bfloat16)
    attended = attended.transpose(2, 0, 1, 3).reshape(tokens_here, kv_local * group_size * HD)
    partial_terms = jnp.dot(attended, out_weight, preferred_element_type=jnp.float32)
    return lax.psum_scatter(
        partial_terms.astype(jnp.bfloat16), "head", scatter_dimension=1, tiled=True
    )


def solution(mesh):
    return jax.shard_map(
        local,
        mesh=mesh,
        in_specs=(P("seq", "head"), P("seq", "head"), P("seq", "head"), P("head", None), P()),
        out_specs=P("seq", "head"),
        check_vma=False,
    )
```

profile of v0, /device:TPU:1, one launch (start us, length us, event | category | flops | bytes accessed | tf_op | source)
XLA Modules:
  0.0 401.6 jit_solution(11792546002265034760)
XLA Ops:
  7.2 97.2 %gather_fusion = s32[16384]{0:T(1024)S(1)} fusion(s32[128]{0:T(128)S(1)} %copy-done, s32[16384]{0:T(1024)S(1)} %broadcast_clamp_fusion), kind=kCustom, calls=%fused_computation | custom fusion | bytes 196608 | tf_op jit(solution)/shard_map/jit(_take)/gather | solution.py:29
  105.5 214.1 %while.21 = (s32[]{:T(128)}, f32[1,4,128]{2,1,0:T(4,128)S(1)}, f32[1,4,128]{2,1,0:T(4,128)S(1)}, f32[1,4,128,128]{3,2,1,0:T(8,128)S(1)}, bf16[2,128,128]{2,1,0:T...) while((s32[]{:T(128)}, f32[1,4,128]{2,1,0:T(4,128)S(1)}, ...), condition=%wide.region_5.6_spmd.clone, body=%wide.region_2.5_spmd.clone.sunk | while | flops 34342664 | bytes 2003221 | solution.py:82
  105.5 4.9 %collective-permute-start = (bf16[2,128,128]{2,1,0:T(8,128)(2,1)S(1)}, bf16[2,128,128]{2,1,0:T(8,128)(2,1)S(1)}, u32[]{:S(2)}, u32[]{:S(2)}) collective-permute-start(bf16[2,128,128]{2,1,0:T(8,128)(2,1)S(1)} %get-tuple-element.347), channel_id=1, source_target_pairs={{0,4},{4,8},{8,12},{12,16},{16,20},{20,24},{24,28},{28,32},{32,36}... | collective-permute-start | bytes 196616 | tf_op jit(solution)/shard_map/while/body/eval_jaxpr/ppermute | solution.py:16
  110.6 3.7 collective-permute-done
  115.0 1.9 collective-permute-start
  117.1 1.1 collective-permute-done
  118.8 4.3 %collective-permute-start = (bf16[2,128,128]{2,1,0:T(8,128)(2,1)S(1)}, bf16[2,128,128]{2,1,0:T(8,128)(2,1)S(1)}, u32[]{:S(2)}, u32[]{:S(2)}) collective-permute-start(bf16[2,128,128]{2,1,0:T(8,128)(2,1)S(1)} %get-tuple-element.347), channel_id=1, source_target_pairs={{0,4},{4,8},{8,12},{12,16},{16,20},{20,24},{24,28},{28,32},{32,36}... | collective-permute-start | bytes 196616 | tf_op jit(solution)/shard_map/while/body/eval_jaxpr/ppermute | solution.py:16
  123.3 1.1 collective-permute-done
  125.0 4.3 %collective-permute-start = (bf16[2,128,128]{2,1,0:T(8,128)(2,1)S(1)}, bf16[2,128,128]{2,1,0:T(8,128)(2,1)S(1)}, u32[]{:S(2)}, u32[]{:S(2)}) collective-permute-start(bf16[2,128,128]{2,1,0:T(8,128)(2,1)S(1)} %get-tuple-element.347), channel_id=1, source_target_pairs={{0,4},{4,8},{8,12},{12,16},{16,20},{20,24},{24,28},{28,32},{32,36}... | collective-permute-start | bytes 196616 | tf_op jit(solution)/shard_map/while/body/eval_jaxpr/ppermute | solution.py:16
  129.5 1.1 collective-permute-done
  131.3 4.3 %collective-permute-start = (bf16[2,128,128]{2,1,0:T(8,128)(2,1)S(1)}, bf16[2,128,128]{2,1,0:T(8,128)(2,1)S(1)}, u32[]{:S(2)}, u32[]{:S(2)}) collective-permute-start(bf16[2,128,128]{2,1,0:T(8,128)(2,1)S(1)} %get-tuple-element.347), channel_id=1, source_target_pairs={{0,4},{4,8},{8,12},{12,16},{16,20},{20,24},{24,28},{28,32},{32,36}... | collective-permute-start | bytes 196616 | tf_op jit(solution)/shard_map/while/body/eval_jaxpr/ppermute | solution.py:16
  135.7 1.1 collective-permute-done
  137.5 4.3 %collective-permute-start = (bf16[2,128,128]{2,1,0:T(8,128)(2,1)S(1)}, bf16[2,128,128]{2,1,0:T(8,128)(2,1)S(1)}, u32[]{:S(2)}, u32[]{:S(2)}) collective-permute-start(bf16[2,128,128]{2,1,0:T(8,128)(2,1)S(1)} %get-tuple-element.347), channel_id=1, source_target_pairs={{0,4},{4,8},{8,12},{12,16},{16,20},{20,24},{24,28},{28,32},{32,36}... | collective-permute-start | bytes 196616 | tf_op jit(solution)/shard_map/while/body/eval_jaxpr/ppermute | solution.py:16
  141.9 1.1 collective-permute-done
  143.7 4.3 %collective-permute-start = (bf16[2,128,128]{2,1,0:T(8,128)(2,1)S(1)}, bf16[2,128,128]{2,1,0:T(8,128)(2,1)S(1)}, u32[]{:S(2)}, u32[]{:S(2)}) collective-permute-start(bf16[2,128,128]{2,1,0:T(8,128)(2,1)S(1)} %get-tuple-element.347), channel_id=1, source_target_pairs={{0,4},{4,8},{8,12},{12,16},{16,20},{20,24},{24,28},{28,32},{32,36}... | collective-permute-start | bytes 196616 | tf_op jit(solution)/shard_map/while/body/eval_jaxpr/ppermute | solution.py:16
  148.2 1.1 collective-permute-done
  149.9 4.3 %collective-permute-start = (bf16[2,128,128]{2,1,0:T(8,128)(2,1)S(1)}, bf16[2,128,128]{2,1,0:T(8,128)(2,1)S(1)}, u32[]{:S(2)}, u32[]{:S(2)}) collective-permute-start(bf16[2,128,128]{2,1,0:T(8,128)(2,1)S(1)} %get-tuple-element.347), channel_id=1, source_target_pairs={{0,4},{4,8},{8,12},{12,16},{16,20},{20,24},{24,28},{28,32},{32,36}... | collective-permute-start | bytes 196616 | tf_op jit(solution)/shard_map/while/body/eval_jaxpr/ppermute | solution.py:16
  154.4 1.1 collective-permute-done
  156.1 4.3 %collective-permute-start = (bf16[2,128,128]{2,1,0:T(8,128)(2,1)S(1)}, bf16[2,128,128]{2,1,0:T(8,128)(2,1)S(1)}, u32[]{:S(2)}, u32[]{:S(2)}) collective-permute-start(bf16[2,128,128]{2,1,0:T(8,128)(2,1)S(1)} %get-tuple-element.347), channel_id=1, source_target_pairs={{0,4},{4,8},{8,12},{12,16},{16,20},{20,24},{24,28},{28,32},{32,36}... | collective-permute-start | bytes 196616 | tf_op jit(solution)/shard_map/while/body/eval_jaxpr/ppermute | solution.py:16
  160.6 1.1 collective-permute-done
  162.3 4.3 %collective-permute-start = (bf16[2,128,128]{2,1,0:T(8,128)(2,1)S(1)}, bf16[2,128,128]{2,1,0:T(8,128)(2,1)S(1)}, u32[]{:S(2)}, u32[]{:S(2)}) collective-permute-start(bf16[2,128,128]{2,1,0:T(8,128)(2,1)S(1)} %get-tuple-element.347), channel_id=1, source_target_pairs={{0,4},{4,8},{8,12},{12,16},{16,20},{20,24},{24,28},{28,32},{32,36}... | collective-permute-start | bytes 196616 | tf_op jit(solution)/shard_map/while/body/eval_jaxpr/ppermute | solution.py:16
  168.5 4.3 %collective-permute-start = (bf16[2,128,128]{2,1,0:T(8,128)(2,1)S(1)}, bf16[2,128,128]{2,1,0:T(8,128)(2,1)S(1)}, u32[]{:S(2)}, u32[]{:S(2)}) collective-permute-start(bf16[2,128,128]{2,1,0:T(8,128)(2,1)S(1)} %get-tuple-element.347), channel_id=1, source_target_pairs={{0,4},{4,8},{8,12},{12,16},{16,20},{20,24},{24,28},{28,32},{32,36}... | collective-permute-start | bytes 196616 | tf_op jit(solution)/shard_map/while/body/eval_jaxpr/ppermute | solution.py:16
  174.7 4.3 %collective-permute-start = (bf16[2,128,128]{2,1,0:T(8,128)(2,1)S(1)}, bf16[2,128,128]{2,1,0:T(8,128)(2,1)S(1)}, u32[]{:S(2)}, u32[]{:S(2)}) collective-permute-start(bf16[2,128,128]{2,1,0:T(8,128)(2,1)S(1)} %get-tuple-element.347), channel_id=1, source_target_pairs={{0,4},{4,8},{8,12},{12,16},{16,20},{20,24},{24,28},{28,32},{32,36}... | collective-permute-start | bytes 196616 | tf_op jit(solution)/shard_map/while/body/eval_jaxpr/ppermute | solution.py:16
  180.9 4.3 %collective-permute-start = (bf16[2,128,128]{2,1,0:T(8,128)(2,1)S(1)}, bf16[2,128,128]{2,1,0:T(8,128)(2,1)S(1)}, u32[]{:S(2)}, u32[]{:S(2)}) collective-permute-start(bf16[2,128,128]{2,1,0:T(8,128)(2,1)S(1)} %get-tuple-element.347), channel_id=1, source_target_pairs={{0,4},{4,8},{8,12},{12,16},{16,20},{20,24},{24,28},{28,32},{32,36}... | collective-permute-start | bytes 196616 | tf_op jit(solution)/shard_map/while/body/eval_jaxpr/ppermute | solution.py:16
  187.2 4.3 %collective-permute-start = (bf16[2,128,128]{2,1,0:T(8,128)(2,1)S(1)}, bf16[2,128,128]{2,1,0:T(8,128)(2,1)S(1)}, u32[]{:S(2)}, u32[]{:S(2)}) collective-permute-start(bf16[2,128,128]{2,1,0:T(8,128)(2,1)S(1)} %get-tuple-element.347), channel_id=1, source_target_pairs={{0,4},{4,8},{8,12},{12,16},{16,20},{20,24},{24,28},{28,32},{32,36}... | collective-permute-start | bytes 196616 | tf_op jit(solution)/shard_map/while/body/eval_jaxpr/ppermute | solution.py:16
  193.4 5.5 %collective-permute-start = (bf16[2,128,128]{2,1,0:T(8,128)(2,1)S(1)}, bf16[2,128,128]{2,1,0:T(8,128)(2,1)S(1)}, u32[]{:S(2)}, u32[]{:S(2)}) collective-permute-start(bf16[2,128,128]{2,1,0:T(8,128)(2,1)S(1)} %get-tuple-element.347), channel_id=1, source_target_pairs={{0,4},{4,8},{8,12},{12,16},{16,20},{20,24},{24,28},{28,32},{32,36}... | collective-permute-start | bytes 196616 | tf_op jit(solution)/shard_map/while/body/eval_jaxpr/ppermute | solution.py:16
  199.1 1.1 collective-permute-done
  200.8 5.5 %collective-permute-start = (bf16[2,128,128]{2,1,0:T(8,128)(2,1)S(1)}, bf16[2,128,128]{2,1,0:T(8,128)(2,1)S(1)}, u32[]{:S(2)}, u32[]{:S(2)}) collective-permute-start(bf16[2,128,128]{2,1,0:T(8,128)(2,1)S(1)} %get-tuple-element.347), channel_id=1, source_target_pairs={{0,4},{4,8},{8,12},{12,16},{16,20},{20,24},{24,28},{28,32},{32,36}... | collective-permute-start | bytes 196616 | tf_op jit(solution)/shard_map/while/body/eval_jaxpr/ppermute | solution.py:16
  208.3 5.5 %collective-permute-start = (bf16[2,128,128]{2,1,0:T(8,128)(2,1)S(1)}, bf16[2,128,128]{2,1,0:T(8,128)(2,1)S(1)}, u32[]{:S(2)}, u32[]{:S(2)}) collective-permute-start(bf16[2,128,128]{2,1,0:T(8,128)(2,1)S(1)} %get-tuple-element.347), channel_id=1, source_target_pairs={{0,4},{4,8},{8,12},{12,16},{16,20},{20,24},{24,28},{28,32},{32,36}... | collective-permute-start | bytes 196616 | tf_op jit(solution)/shard_map/while/body/eval_jaxpr/ppermute | solution.py:16
  215.7 5.5 %collective-permute-start = (bf16[2,128,128]{2,1,0:T(8,128)(2,1)S(1)}, bf16[2,128,128]{2,1,0:T(8,128)(2,1)S(1)}, u32[]{:S(2)}, u32[]{:S(2)}) collective-permute-start(bf16[2,128,128]{2,1,0:T(8,128)(2,1)S(1)} %get-tuple-element.347), channel_id=1, source_target_pairs={{0,4},{4,8},{8,12},{12,16},{16,20},{20,24},{24,28},{28,32},{32,36}... | collective-permute-start | bytes 196616 | tf_op jit(solution)/shard_map/while/body/eval_jaxpr/ppermute | solution.py:16
  221.4 1.1 collective-permute-done
  223.1 5.5 %collective-permute-start = (bf16[2,128,128]{2,1,0:T(8,128)(2,1)S(1)}, bf16[2,128,128]{2,1,0:T(8,128)(2,1)S(1)}, u32[]{:S(2)}, u32[]{:S(2)}) collective-permute-start(bf16[2,128,128]{2,1,0:T(8,128)(2,1)S(1)} %get-tuple-element.347), channel_id=1, source_target_pairs={{0,4},{4,8},{8,12},{12,16},{16,20},{20,24},{24,28},{28,32},{32,36}... | collective-permute-start | bytes 196616 | tf_op jit(solution)/shard_map/while/body/eval_jaxpr/ppermute | solution.py:16
  230.5 5.5 %collective-permute-start = (bf16[2,128,128]{2,1,0:T(8,128)(2,1)S(1)}, bf16[2,128,128]{2,1,0:T(8,128)(2,1)S(1)}, u32[]{:S(2)}, u32[]{:S(2)}) collective-permute-start(bf16[2,128,128]{2,1,0:T(8,128)(2,1)S(1)} %get-tuple-element.347), channel_id=1, source_target_pairs={{0,4},{4,8},{8,12},{12,16},{16,20},{20,24},{24,28},{28,32},{32,36}... | collective-permute-start | bytes 196616 | tf_op jit(solution)/shard_map/while/body/eval_jaxpr/ppermute | solution.py:16
  237.9 5.5 %collective-permute-start = (bf16[2,128,128]{2,1,0:T(8,128)(2,1)S(1)}, bf16[2,128,128]{2,1,0:T(8,128)(2,1)S(1)}, u32[]{:S(2)}, u32[]{:S(2)}) collective-permute-start(bf16[2,128,128]{2,1,0:T(8,128)(2,1)S(1)} %get-tuple-element.347), channel_id=1, source_target_pairs={{0,4},{4,8},{8,12},{12,16},{16,20},{20,24},{24,28},{28,32},{32,36}... | collective-permute-start | bytes 196616 | tf_op jit(solution)/shard_map/while/body/eval_jaxpr/ppermute | solution.py:16
  245.3 5.5 %collective-permute-start = (bf16[2,128,128]{2,1,0:T(8,128)(2,1)S(1)}, bf16[2,128,128]{2,1,0:T(8,128)(2,1)S(1)}, u32[]{:S(2)}, u32[]{:S(2)}) collective-permute-start(bf16[2,128,128]{2,1,0:T(8,128)(2,1)S(1)} %get-tuple-element.347), channel_id=1, source_target_pairs={{0,4},{4,8},{8,12},{12,16},{16,20},{20,24},{24,28},{28,32},{32,36}... | collective-permute-start | bytes 196616 | tf_op jit(solution)/shard_map/while/body/eval_jaxpr/ppermute | solution.py:16
  252.8 5.5 %collective-permute-start = (bf16[2,128,128]{2,1,0:T(8,128)(2,1)S(1)}, bf16[2,128,128]{2,1,0:T(8,128)(2,1)S(1)}, u32[]{:S(2)}, u32[]{:S(2)}) collective-permute-start(bf16[2,128,128]{2,1,0:T(8,128)(2,1)S(1)} %get-tuple-element.347), channel_id=1, source_target_pairs={{0,4},{4,8},{8,12},{12,16},{16,20},{20,24},{24,28},{28,32},{32,36}... | collective-permute-start | bytes 196616 | tf_op jit(solution)/shard_map/while/body/eval_jaxpr/ppermute | solution.py:16
  260.2 5.5 %collective-permute-start = (bf16[2,128,128]{2,1,0:T(8,128)(2,1)S(1)}, bf16[2,128,128]{2,1,0:T(8,128)(2,1)S(1)}, u32[]{:S(2)}, u32[]{:S(2)}) collective-permute-start(bf16[2,128,128]{2,1,0:T(8,128)(2,1)S(1)} %get-tuple-element.347), channel_id=1, source_target_pairs={{0,4},{4,8},{8,12},{12,16},{16,20},{20,24},{24,28},{28,32},{32,36}... | collective-permute-start | bytes 196616 | tf_op jit(solution)/shard_map/while/body/eval_jaxpr/ppermute | solution.py:16
  267.6 5.5 %collective-permute-start = (bf16[2,128,128]{2,1,0:T(8,128)(2,1)S(1)}, bf16[2,128,128]{2,1,0:T(8,128)(2,1)S(1)}, u32[]{:S(2)}, u32[]{:S(2)}) collective-permute-start(bf16[2,128,128]{2,1,0:T(8,128)(2,1)S(1)} %get-tuple-element.347), channel_id=1, source_target_pairs={{0,4},{4,8},{8,12},{12,16},{16,20},{20,24},{24,28},{28,32},{32,36}... | collective-permute-start | bytes 196616 | tf_op jit(solution)/shard_map/while/body/eval_jaxpr/ppermute | solution.py:16
  275.0 5.5 %collective-permute-start = (bf16[2,128,128]{2,1,0:T(8,128)(2,1)S(1)}, bf16[2,128,128]{2,1,0:T(8,128)(2,1)S(1)}, u32[]{:S(2)}, u32[]{:S(2)}) collective-permute-start(bf16[2,128,128]{2,1,0:T(8,128)(2,1)S(1)} %get-tuple-element.347), channel_id=1, source_target_pairs={{0,4},{4,8},{8,12},{12,16},{16,20},{20,24},{24,28},{28,32},{32,36}... | collective-permute-start | bytes 196616 | tf_op jit(solution)/shard_map/while/body/eval_jaxpr/ppermute | solution.py:16
  280.7 1.1 collective-permute-done
  282.4 5.5 %collective-permute-start = (bf16[2,128,128]{2,1,0:T(8,128)(2,1)S(1)}, bf16[2,128,128]{2,1,0:T(8,128)(2,1)S(1)}, u32[]{:S(2)}, u32[]{:S(2)}) collective-permute-start(bf16[2,128,128]{2,1,0:T(8,128)(2,1)S(1)} %get-tuple-element.347), channel_id=1, source_target_pairs={{0,4},{4,8},{8,12},{12,16},{16,20},{20,24},{24,28},{28,32},{32,36}... | collective-permute-start | bytes 196616 | tf_op jit(solution)/shard_map/while/body/eval_jaxpr/ppermute | solution.py:16
  289.9 5.5 %collective-permute-start = (bf16[2,128,128]{2,1,0:T(8,128)(2,1)S(1)}, bf16[2,128,128]{2,1,0:T(8,128)(2,1)S(1)}, u32[]{:S(2)}, u32[]{:S(2)}) collective-permute-start(bf16[2,128,128]{2,1,0:T(8,128)(2,1)S(1)} %get-tuple-element.347), channel_id=1, source_target_pairs={{0,4},{4,8},{8,12},{12,16},{16,20},{20,24},{24,28},{28,32},{32,36}... | collective-permute-start | bytes 196616 | tf_op jit(solution)/shard_map/while/body/eval_jaxpr/ppermute | solution.py:16
  297.3 5.5 %collective-permute-start = (bf16[2,128,128]{2,1,0:T(8,128)(2,1)S(1)}, bf16[2,128,128]{2,1,0:T(8,128)(2,1)S(1)}, u32[]{:S(2)}, u32[]{:S(2)}) collective-permute-start(bf16[2,128,128]{2,1,0:T(8,128)(2,1)S(1)} %get-tuple-element.347), channel_id=1, source_target_pairs={{0,4},{4,8},{8,12},{12,16},{16,20},{20,24},{24,28},{28,32},{32,36}... | collective-permute-start | bytes 196616 | tf_op jit(solution)/shard_map/while/body/eval_jaxpr/ppermute | solution.py:16
  303.0 1.1 collective-permute-done
  304.7 5.5 %collective-permute-start = (bf16[2,128,128]{2,1,0:T(8,128)(2,1)S(1)}, bf16[2,128,128]{2,1,0:T(8,128)(2,1)S(1)}, u32[]{:S(2)}, u32[]{:S(2)}) collective-permute-start(bf16[2,128,128]{2,1,0:T(8,128)(2,1)S(1)} %get-tuple-element.347), channel_id=1, source_target_pairs={{0,4},{4,8},{8,12},{12,16},{16,20},{20,24},{24,28},{28,32},{32,36}... | collective-permute-start | bytes 196616 | tf_op jit(solution)/shard_map/while/body/eval_jaxpr/ppermute | solution.py:16
  312.1 5.5 %collective-permute-start = (bf16[2,128,128]{2,1,0:T(8,128)(2,1)S(1)}, bf16[2,128,128]{2,1,0:T(8,128)(2,1)S(1)}, u32[]{:S(2)}, u32[]{:S(2)}) collective-permute-start(bf16[2,128,128]{2,1,0:T(8,128)(2,1)S(1)} %get-tuple-element.347), channel_id=1, source_target_pairs={{0,4},{4,8},{8,12},{12,16},{16,20},{20,24},{24,28},{28,32},{32,36}... | collective-permute-start | bytes 196616 | tf_op jit(solution)/shard_map/while/body/eval_jaxpr/ppermute | solution.py:16
  319.7 3.9 convolution_convert_fusion
  323.7 71.1 %reduce-scatter.2.cloned.1.call-done = bf16[128,1024]{1,0:T(8,128)(2,1)} async-done(((bf16[128,4096]{1,0:T(8,128)(2,1)}), bf16[128,1024]{1,0:T(8,128)(2,1)}) %reduce-scatter.2.cloned.1.call-update) | async-done | bytes 262160 | tf_op jit(solution)/shard_map/reduce_scatter | solution.py:87
  (355 shorter events, 45.3 us)
Async XLA Ops:
  6.5 0.7 copy-start
  6.5 388.2 %reduce-scatter.2.cloned.1.call-start = ((), (), s32[]{:S(2)}) async-start(), calls=%async_computation.1 | async-start | bytes 1310720 | tf_op jit(solution)/shard_map/reduce_scatter | solution.py:87
  7.2 97.2 %copy-start.1 = (bf16[128,512]{1,0:T(8,128)(2,1)S(1)}, bf16[128,512]{1,0:T(8,128)(2,1)}, u32[]{:S(2)}) copy-start(bf16[128,512]{1,0:T(8,128)(2,1)} %param.9) | copy-start | bytes 393220
  7.2 97.7 %copy-start.2 = (bf16[128,128]{1,0:T(8,128)(2,1)S(1)}, bf16[128,128]{1,0:T(8,128)(2,1)}, u32[]{:S(2)}) copy-start(bf16[128,128]{1,0:T(8,128)(2,1)} %param.10) | copy-start | bytes 98308
  7.2 98.0 %copy-start.3 = (bf16[128,128]{1,0:T(8,128)(2,1)S(1)}, bf16[128,128]{1,0:T(8,128)(2,1)}, u32[]{:S(2)}) copy-start(bf16[128,128]{1,0:T(8,128)(2,1)} %param.11) | copy-start | bytes 98308
  105.5 8.9 %collective-permute-start = (bf16[2,128,128]{2,1,0:T(8,128)(2,1)S(1)}, bf16[2,128,128]{2,1,0:T(8,128)(2,1)S(1)}, u32[]{:S(2)}, u32[]{:S(2)}) collective-permute-start(bf16[2,128,128]{2,1,0:T(8,128)(2,1)S(1)} %get-tuple-element.347), channel_id=1, source_target_pairs={{0,4},{4,8},{8,12},{12,16},{16,20},{20,24},{24,28},{28,32},{32,36}... | collective-permute-start | bytes 196616 | tf_op jit(solution)/shard_map/while/body/eval_jaxpr/ppermute | solution.py:16
  115.0 3.2 collective-permute-start
  118.8 5.6 %collective-permute-start = (bf16[2,128,128]{2,1,0:T(8,128)(2,1)S(1)}, bf16[2,128,128]{2,1,0:T(8,128)(2,1)S(1)}, u32[]{:S(2)}, u32[]{:S(2)}) collective-permute-start(bf16[2,128,128]{2,1,0:T(8,128)(2,1)S(1)} %get-tuple-element.347), channel_id=1, source_target_pairs={{0,4},{4,8},{8,12},{12,16},{16,20},{20,24},{24,28},{28,32},{32,36}... | collective-permute-start | bytes 196616 | tf_op jit(solution)/shard_map/while/body/eval_jaxpr/ppermute | solution.py:16
  125.0 5.6 %collective-permute-start = (bf16[2,128,128]{2,1,0:T(8,128)(2,1)S(1)}, bf16[2,128,128]{2,1,0:T(8,128)(2,1)S(1)}, u32[]{:S(2)}, u32[]{:S(2)}) collective-permute-start(bf16[2,128,128]{2,1,0:T(8,128)(2,1)S(1)} %get-tuple-element.347), channel_id=1, source_target_pairs={{0,4},{4,8},{8,12},{12,16},{16,20},{20,24},{24,28},{28,32},{32,36}... | collective-permute-start | bytes 196616 | tf_op jit(solution)/shard_map/while/body/eval_jaxpr/ppermute | solution.py:16
  131.3 5.6 %collective-permute-start = (bf16[2,128,128]{2,1,0:T(8,128)(2,1)S(1)}, bf16[2,128,128]{2,1,0:T(8,128)(2,1)S(1)}, u32[]{:S(2)}, u32[]{:S(2)}) collective-permute-start(bf16[2,128,128]{2,1,0:T(8,128)(2,1)S(1)} %get-tuple-element.347), channel_id=1, source_target_pairs={{0,4},{4,8},{8,12},{12,16},{16,20},{20,24},{24,28},{28,32},{32,36}... | collective-permute-start | bytes 196616 | tf_op jit(solution)/shard_map/while/body/eval_jaxpr/ppermute | solution.py:16
  137.5 5.6 %collective-permute-start = (bf16[2,128,128]{2,1,0:T(8,128)(2,1)S(1)}, bf16[2,128,128]{2,1,0:T(8,128)(2,1)S(1)}, u32[]{:S(2)}, u32[]{:S(2)}) collective-permute-start(bf16[2,128,128]{2,1,0:T(8,128)(2,1)S(1)} %get-tuple-element.347), channel_id=1, source_target_pairs={{0,4},{4,8},{8,12},{12,16},{16,20},{20,24},{24,28},{28,32},{32,36}... | collective-permute-start | bytes 196616 | tf_op jit(solution)/shard_map/while/body/eval_jaxpr/ppermute | solution.py:16
  143.7 5.6 %collective-permute-start = (bf16[2,128,128]{2,1,0:T(8,128)(2,1)S(1)}, bf16[2,128,128]{2,1,0:T(8,128)(2,1)S(1)}, u32[]{:S(2)}, u32[]{:S(2)}) collective-permute-start(bf16[2,128,128]{2,1,0:T(8,128)(2,1)S(1)} %get-tuple-element.347), channel_id=1, source_target_pairs={{0,4},{4,8},{8,12},{12,16},{16,20},{20,24},{24,28},{28,32},{32,36}... | collective-permute-start | bytes 196616 | tf_op jit(solution)/shard_map/while/body/eval_jaxpr/ppermute | solution.py:16
  149.9 5.6 %collective-permute-start = (bf16[2,128,128]{2,1,0:T(8,128)(2,1)S(1)}, bf16[2,128,128]{2,1,0:T(8,128)(2,1)S(1)}, u32[]{:S(2)}, u32[]{:S(2)}) collective-permute-start(bf16[2,128,128]{2,1,0:T(8,128)(2,1)S(1)} %get-tuple-element.347), channel_id=1, source_target_pairs={{0,4},{4,8},{8,12},{12,16},{16,20},{20,24},{24,28},{28,32},{32,36}... | collective-permute-start | bytes 196616 | tf_op jit(solution)/shard_map/while/body/eval_jaxpr/ppermute | solution.py:16
  156.1 5.6 %collective-permute-start = (bf16[2,128,128]{2,1,0:T(8,128)(2,1)S(1)}, bf16[2,128,128]{2,1,0:T(8,128)(2,1)S(1)}, u32[]{:S(2)}, u32[]{:S(2)}) collective-permute-start(bf16[2,128,128]{2,1,0:T(8,128)(2,1)S(1)} %get-tuple-element.347), channel_id=1, source_target_pairs={{0,4},{4,8},{8,12},{12,16},{16,20},{20,24},{24,28},{28,32},{32,36}... | collective-permute-start | bytes 196616 | tf_op jit(solution)/shard_map/while/body/eval_jaxpr/ppermute | solution.py:16
  162.3 5.6 %collective-permute-start = (bf16[2,128,128]{2,1,0:T(8,128)(2,1)S(1)}, bf16[2,128,128]{2,1,0:T(8,128)(2,1)S(1)}, u32[]{:S(2)}, u32[]{:S(2)}) collective-permute-start(bf16[2,128,128]{2,1,0:T(8,128)(2,1)S(1)} %get-tuple-element.347), channel_id=1, source_target_pairs={{0,4},{4,8},{8,12},{12,16},{16,20},{20,24},{24,28},{28,32},{32,36}... | collective-permute-start | bytes 196616 | tf_op jit(solution)/shard_map/while/body/eval_jaxpr/ppermute | solution.py:16
  168.5 5.6 %collective-permute-start = (bf16[2,128,128]{2,1,0:T(8,128)(2,1)S(1)}, bf16[2,128,128]{2,1,0:T(8,128)(2,1)S(1)}, u32[]{:S(2)}, u32[]{:S(2)}) collective-permute-start(bf16[2,128,128]{2,1,0:T(8,128)(2,1)S(1)} %get-tuple-element.347), channel_id=1, source_target_pairs={{0,4},{4,8},{8,12},{12,16},{16,20},{20,24},{24,28},{28,32},{32,36}... | collective-permute-start | bytes 196616 | tf_op jit(solution)/shard_map/while/body/eval_jaxpr/ppermute | solution.py:16
  174.7 5.6 %collective-permute-start = (bf16[2,128,128]{2,1,0:T(8,128)(2,1)S(1)}, bf16[2,128,128]{2,1,0:T(8,128)(2,1)S(1)}, u32[]{:S(2)}, u32[]{:S(2)}) collective-permute-start(bf16[2,128,128]{2,1,0:T(8,128)(2,1)S(1)} %get-tuple-element.347), channel_id=1, source_target_pairs={{0,4},{4,8},{8,12},{12,16},{16,20},{20,24},{24,28},{28,32},{32,36}... | collective-permute-start | bytes 196616 | tf_op jit(solution)/shard_map/while/body/eval_jaxpr/ppermute | solution.py:16
  180.9 5.6 %collective-permute-start = (bf16[2,128,128]{2,1,0:T(8,128)(2,1)S(1)}, bf16[2,128,128]{2,1,0:T(8,128)(2,1)S(1)}, u32[]{:S(2)}, u32[]{:S(2)}) collective-permute-start(bf16[2,128,128]{2,1,0:T(8,128)(2,1)S(1)} %get-tuple-element.347), channel_id=1, source_target_pairs={{0,4},{4,8},{8,12},{12,16},{16,20},{20,24},{24,28},{28,32},{32,36}... | collective-permute-start | bytes 196616 | tf_op jit(solution)/shard_map/while/body/eval_jaxpr/ppermute | solution.py:16
  187.2 5.6 %collective-permute-start = (bf16[2,128,128]{2,1,0:T(8,128)(2,1)S(1)}, bf16[2,128,128]{2,1,0:T(8,128)(2,1)S(1)}, u32[]{:S(2)}, u32[]{:S(2)}) collective-permute-start(bf16[2,128,128]{2,1,0:T(8,128)(2,1)S(1)} %get-tuple-element.347), channel_id=1, source_target_pairs={{0,4},{4,8},{8,12},{12,16},{16,20},{20,24},{24,28},{28,32},{32,36}... | collective-permute-start | bytes 196616 | tf_op jit(solution)/shard_map/while/body/eval_jaxpr/ppermute | solution.py:16
  193.4 6.8 %collective-permute-start = (bf16[2,128,128]{2,1,0:T(8,128)(2,1)S(1)}, bf16[2,128,128]{2,1,0:T(8,128)(2,1)S(1)}, u32[]{:S(2)}, u32[]{:S(2)}) collective-permute-start(bf16[2,128,128]{2,1,0:T(8,128)(2,1)S(1)} %get-tuple-element.347), channel_id=1, source_target_pairs={{0,4},{4,8},{8,12},{12,16},{16,20},{20,24},{24,28},{28,32},{32,36}... | collective-permute-start | bytes 196616 | tf_op jit(solution)/shard_map/while/body/eval_jaxpr/ppermute | solution.py:16
  200.8 6.8 %collective-permute-start = (bf16[2,128,128]{2,1,0:T(8,128)(2,1)S(1)}, bf16[2,128,128]{2,1,0:T(8,128)(2,1)S(1)}, u32[]{:S(2)}, u32[]{:S(2)}) collective-permute-start(bf16[2,128,128]{2,1,0:T(8,128)(2,1)S(1)} %get-tuple-element.347), channel_id=1, source_target_pairs={{0,4},{4,8},{8,12},{12,16},{16,20},{20,24},{24,28},{28,32},{32,36}... | collective-permute-start | bytes 196616 | tf_op jit(solution)/shard_map/while/body/eval_jaxpr/ppermute | solution.py:16
  208.3 6.8 %collective-permute-start = (bf16[2,128,128]{2,1,0:T(8,128)(2,1)S(1)}, bf16[2,128,128]{2,1,0:T(8,128)(2,1)S(1)}, u32[]{:S(2)}, u32[]{:S(2)}) collective-permute-start(bf16[2,128,128]{2,1,0:T(8,128)(2,1)S(1)} %get-tuple-element.347), channel_id=1, source_target_pairs={{0,4},{4,8},{8,12},{12,16},{16,20},{20,24},{24,28},{28,32},{32,36}... | collective-permute-start | bytes 196616 | tf_op jit(solution)/shard_map/while/body/eval_jaxpr/ppermute | solution.py:16
  215.7 6.8 %collective-permute-start = (bf16[2,128,128]{2,1,0:T(8,128)(2,1)S(1)}, bf16[2,128,128]{2,1,0:T(8,128)(2,1)S(1)}, u32[]{:S(2)}, u32[]{:S(2)}) collective-permute-start(bf16[2,128,128]{2,1,0:T(8,128)(2,1)S(1)} %get-tuple-element.347), channel_id=1, source_target_pairs={{0,4},{4,8},{8,12},{12,16},{16,20},{20,24},{24,28},{28,32},{32,36}... | collective-permute-start | bytes 196616 | tf_op jit(solution)/shard_map/while/body/eval_jaxpr/ppermute | solution.py:16
  223.1 6.8 %collective-permute-start = (bf16[2,128,128]{2,1,0:T(8,128)(2,1)S(1)}, bf16[2,128,128]{2,1,0:T(8,128)(2,1)S(1)}, u32[]{:S(2)}, u32[]{:S(2)}) collective-permute-start(bf16[2,128,128]{2,1,0:T(8,128)(2,1)S(1)} %get-tuple-element.347), channel_id=1, source_target_pairs={{0,4},{4,8},{8,12},{12,16},{16,20},{20,24},{24,28},{28,32},{32,36}... | collective-permute-start | bytes 196616 | tf_op jit(solution)/shard_map/while/body/eval_jaxpr/ppermute | solution.py:16
  230.5 6.8 %collective-permute-start = (bf16[2,128,128]{2,1,0:T(8,128)(2,1)S(1)}, bf16[2,128,128]{2,1,0:T(8,128)(2,1)S(1)}, u32[]{:S(2)}, u32[]{:S(2)}) collective-permute-start(bf16[2,128,128]{2,1,0:T(8,128)(2,1)S(1)} %get-tuple-element.347), channel_id=1, source_target_pairs={{0,4},{4,8},{8,12},{12,16},{16,20},{20,24},{24,28},{28,32},{32,36}... | collective-permute-start | bytes 196616 | tf_op jit(solution)/shard_map/while/body/eval_jaxpr/ppermute | solution.py:16
  237.9 6.8 %collective-permute-start = (bf16[2,128,128]{2,1,0:T(8,128)(2,1)S(1)}, bf16[2,128,128]{2,1,0:T(8,128)(2,1)S(1)}, u32[]{:S(2)}, u32[]{:S(2)}) collective-permute-start(bf16[2,128,128]{2,1,0:T(8,128)(2,1)S(1)} %get-tuple-element.347), channel_id=1, source_target_pairs={{0,4},{4,8},{8,12},{12,16},{16,20},{20,24},{24,28},{28,32},{32,36}... | collective-permute-start | bytes 196616 | tf_op jit(solution)/shard_map/while/body/eval_jaxpr/ppermute | solution.py:16
  245.3 6.8 %collective-permute-start = (bf16[2,128,128]{2,1,0:T(8,128)(2,1)S(1)}, bf16[2,128,128]{2,1,0:T(8,128)(2,1)S(1)}, u32[]{:S(2)}, u32[]{:S(2)}) collective-permute-start(bf16[2,128,128]{2,1,0:T(8,128)(2,1)S(1)} %get-tuple-element.347), channel_id=1, source_target_pairs={{0,4},{4,8},{8,12},{12,16},{16,20},{20,24},{24,28},{28,32},{32,36}... | collective-permute-start | bytes 196616 | tf_op jit(solution)/shard_map/while/body/eval_jaxpr/ppermute | solution.py:16
  252.8 6.8 %collective-permute-start = (bf16[2,128,128]{2,1,0:T(8,128)(2,1)S(1)}, bf16[2,128,128]{2,1,0:T(8,128)(2,1)S(1)}, u32[]{:S(2)}, u32[]{:S(2)}) collective-permute-start(bf16[2,128,128]{2,1,0:T(8,128)(2,1)S(1)} %get-tuple-element.347), channel_id=1, source_target_pairs={{0,4},{4,8},{8,12},{12,16},{16,20},{20,24},{24,28},{28,32},{32,36}... | collective-permute-start | bytes 196616 | tf_op jit(solution)/shard_map/while/body/eval_jaxpr/ppermute | solution.py:16
  260.2 6.8 %collective-permute-start = (bf16[2,128,128]{2,1,0:T(8,128)(2,1)S(1)}, bf16[2,128,128]{2,1,0:T(8,128)(2,1)S(1)}, u32[]{:S(2)}, u32[]{:S(2)}) collective-permute-start(bf16[2,128,128]{2,1,0:T(8,128)(2,1)S(1)} %get-tuple-element.347), channel_id=1, source_target_pairs={{0,4},{4,8},{8,12},{12,16},{16,20},{20,24},{24,28},{28,32},{32,36}... | collective-permute-start | bytes 196616 | tf_op jit(solution)/shard_map/while/body/eval_jaxpr/ppermute | solution.py:16
  267.6 6.8 %collective-permute-start = (bf16[2,128,128]{2,1,0:T(8,128)(2,1)S(1)}, bf16[2,128,128]{2,1,0:T(8,128)(2,1)S(1)}, u32[]{:S(2)}, u32[]{:S(2)}) collective-permute-start(bf16[2,128,128]{2,1,0:T(8,128)(2,1)S(1)} %get-tuple-element.347), channel_id=1, source_target_pairs={{0,4},{4,8},{8,12},{12,16},{16,20},{20,24},{24,28},{28,32},{32,36}... | collective-permute-start | bytes 196616 | tf_op jit(solution)/shard_map/while/body/eval_jaxpr/ppermute | solution.py:16
  275.0 6.8 %collective-permute-start = (bf16[2,128,128]{2,1,0:T(8,128)(2,1)S(1)}, bf16[2,128,128]{2,1,0:T(8,128)(2,1)S(1)}, u32[]{:S(2)}, u32[]{:S(2)}) collective-permute-start(bf16[2,128,128]{2,1,0:T(8,128)(2,1)S(1)} %get-tuple-element.347), channel_id=1, source_target_pairs={{0,4},{4,8},{8,12},{12,16},{16,20},{20,24},{24,28},{28,32},{32,36}... | collective-permute-start | bytes 196616 | tf_op jit(solution)/shard_map/while/body/eval_jaxpr/ppermute | solution.py:16
  282.4 6.8 %collective-permute-start = (bf16[2,128,128]{2,1,0:T(8,128)(2,1)S(1)}, bf16[2,128,128]{2,1,0:T(8,128)(2,1)S(1)}, u32[]{:S(2)}, u32[]{:S(2)}) collective-permute-start(bf16[2,128,128]{2,1,0:T(8,128)(2,1)S(1)} %get-tuple-element.347), channel_id=1, source_target_pairs={{0,4},{4,8},{8,12},{12,16},{16,20},{20,24},{24,28},{28,32},{32,36}... | collective-permute-start | bytes 196616 | tf_op jit(solution)/shard_map/while/body/eval_jaxpr/ppermute | solution.py:16
  289.9 6.8 %collective-permute-start = (bf16[2,128,128]{2,1,0:T(8,128)(2,1)S(1)}, bf16[2,128,128]{2,1,0:T(8,128)(2,1)S(1)}, u32[]{:S(2)}, u32[]{:S(2)}) collective-permute-start(bf16[2,128,128]{2,1,0:T(8,128)(2,1)S(1)} %get-tuple-element.347), channel_id=1, source_target_pairs={{0,4},{4,8},{8,12},{12,16},{16,20},{20,24},{24,28},{28,32},{32,36}... | collective-permute-start | bytes 196616 | tf_op jit(solution)/shard_map/while/body/eval_jaxpr/ppermute | solution.py:16
  297.3 6.8 %collective-permute-start = (bf16[2,128,128]{2,1,0:T(8,128)(2,1)S(1)}, bf16[2,128,128]{2,1,0:T(8,128)(2,1)S(1)}, u32[]{:S(2)}, u32[]{:S(2)}) collective-permute-start(bf16[2,128,128]{2,1,0:T(8,128)(2,1)S(1)} %get-tuple-element.347), channel_id=1, source_target_pairs={{0,4},{4,8},{8,12},{12,16},{16,20},{20,24},{24,28},{28,32},{32,36}... | collective-permute-start | bytes 196616 | tf_op jit(solution)/shard_map/while/body/eval_jaxpr/ppermute | solution.py:16
  304.7 6.8 %collective-permute-start = (bf16[2,128,128]{2,1,0:T(8,128)(2,1)S(1)}, bf16[2,128,128]{2,1,0:T(8,128)(2,1)S(1)}, u32[]{:S(2)}, u32[]{:S(2)}) collective-permute-start(bf16[2,128,128]{2,1,0:T(8,128)(2,1)S(1)} %get-tuple-element.347), channel_id=1, source_target_pairs={{0,4},{4,8},{8,12},{12,16},{16,20},{20,24},{24,28},{28,32},{32,36}... | collective-permute-start | bytes 196616 | tf_op jit(solution)/shard_map/while/body/eval_jaxpr/ppermute | solution.py:16
  312.1 6.8 %collective-permute-start = (bf16[2,128,128]{2,1,0:T(8,128)(2,1)S(1)}, bf16[2,128,128]{2,1,0:T(8,128)(2,1)S(1)}, u32[]{:S(2)}, u32[]{:S(2)}) collective-permute-start(bf16[2,128,128]{2,1,0:T(8,128)(2,1)S(1)} %get-tuple-element.347), channel_id=1, source_target_pairs={{0,4},{4,8},{8,12},{12,16},{16,20},{20,24},{24,28},{28,32},{32,36}... | collective-permute-start | bytes 196616 | tf_op jit(solution)/shard_map/while/body/eval_jaxpr/ppermute | solution.py:16
Sparse Core Ops, SparseCore 0:
  323.8 70.9 reduce-scatter.1
where the time goes:
time: 409 us; the launch traced here: 402 us
  starting transfers between devices  151 us (37%)
  waiting for transfers between devices  108 us (26%)
  local copies, waits for them, and re-layouts  101 us (25%)
  matrix products  19.2 us (5%)
  between operations  13.5 us (3%)
  other arithmetic  6.59 us (2%)
    ppermute x31, starting transfers between devices, passed_along(): lax.ppermute(value, axis, [(source, source + steps) for source in range(i...  151 us
    gather x1, local copies, waits for them, and re-layouts, local(): jnp.repeat(block_docs, BLK, total_repeat_length=block_count * BLK)  97.2 us
    reduce_scatter x1, waiting for transfers between devices, local(): lax.psum_scatter(partial_terms.astype(jnp.bfloat16), 'head', scatter_dime...  71.1 us
    ppermute x31, waiting for transfers between devices, passed_along(): lax.ppermute(value, axis, [(source, source + steps) for source in range(i...  36.8 us
    dot_general x32, matrix products, absorb(): jnp.einsum('qnuh,hqm->qnum', weights.astype(jnp.bfloat16), value_shard.re...  8.75 us
  transfers between devices with their start and end apart: 32, of which 32 were waited for; matrix products, arithmetic and copies ran while one was open for 1% of the time, Pallas kernels for 0%

commit v1 on v0

v1 whole, which is shorter than its diff:
```python
import functools

import jax
import jax.numpy as jnp
from jax import lax
from jax.experimental import pallas as pl
from jax.experimental.pallas import tpu as pltpu
from jax.sharding import PartitionSpec as P

HD = 128
BLK = 128
GROUP = 4
HOPS = 8
JUMP = 4 * HOPS
COEF = 1.4426950408889634 / HD**0.5
FAR = 1e30
MESH = pl.DeviceIdType.MESH


def kernel(
    docs, q_hbm, k_hbm, v_hbm, w_hbm, out,
    q_in, qs, kb, vb, wv, acc, row_max, row_sum, att,
    p_out, p_in,
    loc_sem, send_sem, recv_sem, rs_send, rs_recv,
):
    s = lax.axis_index("seq")
    y = lax.axis_index("head")
    n = lax.axis_size("seq")
    heads = lax.axis_size("head")
    rows = BLK * GROUP
    width = wv.shape[2]
    half = width // 2
    fwd = lax.rem(s + 2, n)
    bwd = lax.rem(s + n - 2, n)
    far = lax.rem(s + JUMP, n)
    near = lax.rem(s + n - JUMP, n)
    mate = s + 1 - 2 * lax.rem(s, 2)
    up = lax.rem(y + 1, heads)
    down = lax.rem(y + heads - 1, heads)
    across = lax.rem(y + 2, heads)

    k_load = pltpu.make_async_copy(k_hbm, kb.at[0], loc_sem.at[0])
    v_load = pltpu.make_async_copy(v_hbm, vb.at[0], loc_sem.at[1])
    q_load = pltpu.make_async_copy(q_hbm, q_in, loc_sem.at[2])
    k_load.start()
    v_load.start()
    q_load.start()

    barrier = pltpu.get_barrier_semaphore()
    for peer in (fwd, bwd, far, near, mate):
        pl.semaphore_signal(barrier, inc=1, device_id={"seq": peer}, device_id_type=MESH)
    for peer in (up, down):
        pl.semaphore_signal(barrier, inc=1, device_id={"head": peer}, device_id_type=MESH)

    w_loads = []
    for i, dest in enumerate((across, up, down, y)):
        columns = pl.ds(pl.multiple_of(dest * width, width), width)
        load = pltpu.make_async_copy(w_hbm.at[:, columns], wv.at[i], loc_sem.at[3 + i])
        load.start()
        w_loads.append(load)
    pl.semaphore_wait(barrier, 7)

    def hop(t, kind, part):
        buf = (kb, vb)[part]
        if kind in (0, 2) or (isinstance(t, int) and t == 0):
            src = 4 * t
        else:
            src = 4 * t + 1
        if kind == 0:
            peer = fwd
        elif kind == 1:
            peer = far if (isinstance(t, int) and t == 0) else bwd
        else:
            peer = mate
        return pltpu.make_async_remote_copy(
            src_ref=buf.at[src],
            dst_ref=buf.at[4 * (t + 1) + kind],
            send_sem=send_sem.at[t, kind, part],
            recv_sem=recv_sem.at[t + 1, kind, part],
            device_id={"seq": peer},
            device_id_type=MESH,
        )

    def penalty(distance):
        other = s - distance
        same = docs[jnp.maximum(other, 0)] == docs[s]
        return jnp.where(same & (other >= 0) & (distance > 0), 0.0, FAR).astype(jnp.float32)

    def absorb(first, count, penalties):
        keys = kb[pl.ds(first, count)].reshape(count * BLK, HD)
        values = vb[pl.ds(first, count)].reshape(count * BLK, HD)
        scores = lax.dot_general(
            keys, qs[...], (((1,), (1,)), ((), ())), preferred_element_type=jnp.float32
        )
        parts = [scores[i * BLK:(i + 1) * BLK] for i in range(count)]
        old = row_max[...]
        new = old
        for part, pen in zip(parts, penalties):
            new = jnp.maximum(new, jnp.max(part, axis=0, keepdims=True) - pen)
        factor = jnp.exp2((old - new) * COEF)
        total = row_sum[...] * factor
        weights = []
        for part, pen in zip(parts, penalties):
            weight = jnp.exp2((part - (new + pen)) * COEF)
            total = total + jnp.sum(weight, axis=0, keepdims=True)
            weights.append(weight.astype(jnp.bfloat16))
        product = lax.dot_general(
            values, jnp.concatenate(weights, axis=0), (((0,), (0,)), ((), ())),
            preferred_element_type=jnp.float32,
        )
        acc[...] = acc[...] * factor + product
        row_max[...] = new
        row_sum[...] = total

    k_load.wait()
    for kind in (0, 1, 2):
        hop(0, kind, 0).start()
    v_load.wait()
    for kind in (0, 1, 2):
        hop(0, kind, 1).start()

    q_load.wait()
    for g in range(GROUP):
        qs[g * BLK:(g + 1) * BLK, :] = q_in[:, g * HD:(g + 1) * HD]

    scores = lax.dot_general(
        kb[0], qs[...], (((1,), (1,)), ((), ())), preferred_element_type=jnp.float32
    )
    key_at = lax.broadcasted_iota(jnp.int32, (BLK, rows), 0)
    query_at = lax.rem(lax.broadcasted_iota(jnp.int32, (BLK, rows), 1), BLK)
    scores = jnp.where(key_at <= query_at, scores, -FAR)
    top = jnp.max(scores, axis=0, keepdims=True)
    weight = jnp.exp2((scores - top) * COEF)
    row_max[...] = top
    row_sum[...] = jnp.sum(weight, axis=0, keepdims=True)
    acc[...] = lax.dot_general(
        vb[0], weight.astype(jnp.bfloat16), (((0,), (0,)), ((), ())),
        preferred_element_type=jnp.float32,
    )

    skew = 2 * lax.rem(s, 2) - 1

    def arrive(t, kinds, onward):
        for part in (0, 1):
            for kind in kinds:
                hop(t - 1, kind, part).wait_recv()
                if onward:
                    hop(t, kind, part).start()
                hop(t, kind + 2, part).start()

    arrive(1, (0, 1), True)
    for part in (0, 1):
        hop(0, 2, part).wait_recv()
    absorb(4, 3, [penalty(2), penalty(4 * HOPS), penalty(skew)])

    def middle(t, onward):
        arrive(t, (0, 1), onward)
        for part in (0, 1):
            for kind in (2, 3):
                hop(t - 1, kind, part).wait_recv()
        absorb(
            4 * t, 4,
            [
                penalty(2 * t),
                penalty(4 * HOPS + 2 - 2 * t),
                penalty(2 * (t - 1) + skew),
                penalty(4 * HOPS + 4 - 2 * t + skew),
            ],
        )

    @pl.loop(2, HOPS)
    def _(t):
        middle(t, True)

    middle(HOPS, False)
    for part in (0, 1):
        for kind in (2, 3):
            hop(HOPS, kind, part).wait_recv()
    absorb(
        4 * (HOPS + 1) + 2, 2,
        [penalty(2 * HOPS + skew), penalty(2 * HOPS + 2 + skew)],
    )

    scaled = acc[...] / row_sum[...]
    for g in range(GROUP):
        att[:, g * HD:(g + 1) * HD] = scaled[:, g * BLK:(g + 1) * BLK].T.astype(jnp.bfloat16)

    def project(i, side):
        return jnp.dot(
            att[...], wv[i, :, side * half:(side + 1) * half],
            preferred_element_type=jnp.float32,
        )

    def give(stage, side):
        return pltpu.make_async_remote_copy(
            src_ref=p_out.at[stage, side],
            dst_ref=p_in.at[stage, side],
            send_sem=rs_send.at[stage, side],
            recv_sem=rs_recv.at[stage, side],
            device_id={"head": up if side == 0 else down},
            device_id_type=MESH,
        )

    w_loads[0].wait()
    for side in (0, 1):
        p_out[0, side] = project(0, side).astype(jnp.bfloat16)
        give(0, side).start()
    w_loads[1].wait()
    w_loads[2].wait()
    for side in (0, 1):
        p_out[1, side] = project(1 + side, 1 - side).astype(jnp.bfloat16)
        give(1, side).start()
    held = [project(1 + side, side) for side in (0, 1)]
    for side in (0, 1):
        give(0, side).wait_recv()
        p_out[2, side] = (held[side] + p_in[0, side].astype(jnp.float32)).astype(jnp.bfloat16)
        give(2, side).start()
    w_loads[3].wait()
    own = [project(3, side) for side in (0, 1)]
    for side in (0, 1):
        give(1, 1 - side).wait_recv()
        own[side] = own[side] + p_in[1, 1 - side].astype(jnp.float32)
    for side in (0, 1):
        give(2, side).wait_recv()
        out[:, side * half:(side + 1) * half] = (
            own[side] + p_in[2, side].astype(jnp.float32)
        ).astype(jnp.bfloat16)

    for part in (0, 1):
        for kind in (0, 1, 2):
            hop(0, kind, part).wait_send()

    @pl.loop(1, HOPS)
    def _(t):
        for part in (0, 1):
            for kind in (0, 1, 2, 3):
                hop(t, kind, part).wait_send()

    for part in (0, 1):
        for kind in (2, 3):
            hop(HOPS, kind, part).wait_send()
    for stage in (0, 1, 2):
        for side in (0, 1):
            give(stage, side).wait_send()


def local(query_states, key_states, value_states, out_weight, block_docs):
    tokens = query_states.shape[0]
    model = out_weight.shape[1]
    width = model // lax.axis_size("head")
    rows = GROUP * BLK
    any_space = pl.BlockSpec(memory_space=pl.ANY)
    return pl.pallas_call(
        kernel,
        out_shape=jax.ShapeDtypeStruct((tokens, width), jnp.bfloat16),
        in_specs=[pl.BlockSpec(memory_space=pltpu.SMEM)] + [any_space] * 4,
        out_specs=pl.BlockSpec(memory_space=pltpu.VMEM),
        scratch_shapes=[
            pltpu.VMEM((tokens, rows), jnp.bfloat16),
            pltpu.VMEM((rows, HD), jnp.bfloat16),
            pltpu.VMEM((4 * (HOPS + 2), BLK, HD), jnp.bfloat16),
            pltpu.VMEM((4 * (HOPS + 2), BLK, HD), jnp.bfloat16),
            pltpu.VMEM((4, rows, width), jnp.bfloat16),
            pltpu.VMEM((HD, rows), jnp.float32),
            pltpu.VMEM((1, rows), jnp.float32),
            pltpu.VMEM((1, rows), jnp.float32),
            pltpu.VMEM((tokens, rows), jnp.bfloat16),
            pltpu.VMEM((3, 2, tokens, width // 2), jnp.bfloat16),
            pltpu.VMEM((3, 2, tokens, width // 2), jnp.bfloat16),
            pltpu.SemaphoreType.DMA((7,)),
            pltpu.SemaphoreType.DMA((HOPS + 1, 4, 2)),
            pltpu.SemaphoreType.DMA((HOPS + 2, 4, 2)),
            pltpu.SemaphoreType.DMA((3, 2)),
            pltpu.SemaphoreType.DMA((3, 2)),
        ],
        compiler_params=pltpu.CompilerParams(
            collective_id=0, has_side_effects=True, vmem_limit_bytes=60 << 20
        ),
    )(block_docs, query_states, key_states, value_states, out_weight)


def solution(mesh):
    return jax.shard_map(
        local,
        mesh=mesh,
        in_specs=(P("seq", "head"), P("seq", "head"), P("seq", "head"), P("head", None), P()),
        out_specs=P("seq", "head"),
        check_vma=False,
    )
```

time: 409 us -> 65.4 us (0.16); the launches traced: 402 us -> 65.2 us
  starting transfers between devices: 151 us -> 0 us
  waiting for transfers between devices: 108 us -> 0 us
  local copies, waits for them, and re-layouts: 101 us -> 1.67 us
  Pallas kernels: 0 us -> 63.6 us
  matrix products: 19.2 us -> 0 us
  between operations: 13.5 us -> 0.01 us
  other arithmetic: 6.59 us -> 0 us
    ppermute x31 -> x0, starting transfers between devices: 151 us -> none  [passed_along(): lax.ppermute(value, axis, [(source, source + steps) for source in range(i...]
    gather x1 -> x0, local copies, waits for them, and re-layouts: 97.2 us -> none  [local(): jnp.repeat(block_docs, BLK, total_repeat_length=block_count * BLK)]
    reduce_scatter x1 -> x0, waiting for transfers between devices: 71.1 us -> none  [local(): lax.psum_scatter(partial_terms.astype(jnp.bfloat16), 'head', scatter_dime...]
    pallas_call x0 -> x1, Pallas kernels: none -> 63.6 us  [local(): pl.pallas_call(kernel, out_shape=jax.ShapeDtypeStruct((tokens, width), jn...]
    ppermute x31 -> x0, waiting for transfers between devices: 36.8 us -> none  [passed_along(): lax.ppermute(value, axis, [(source, source + steps) for source in range(i...]
    dot_general x65 -> x0, matrix products: 19.2 us -> none  [the longest x32 8.75 us: absorb(): jnp.einsum('qnuh,hqm->qnum', weights.astype(jnp.bfloat16), value_shard.re...]
  transfers between devices with their start and end apart: 32 -> 0, of which waited for: 32 -> 0; matrix products, arithmetic and copies ran while one was open for 1% -> 0% of each run, Pallas kernels for 0% -> 0%
where the time goes in v1:
time: 65.4 us; the launch traced here: 65.2 us
  Pallas kernels  63.6 us (97%)
  local copies, waits for them, and re-layouts  1.67 us (3%)
    pallas_call x1, Pallas kernels, local(): pl.pallas_call(kernel, out_shape=jax.ShapeDtypeStruct((tokens, width), jn...  63.6 us
    unnamed x1, local copies, waits for them, and re-layouts  1.67 us

profile of v1, /device:TPU:1, one launch (start us, length us, event | category | flops | bytes accessed | tf_op | source)
XLA Modules:
  0.0 65.2 jit_solution(1659818616789134848)
XLA Ops:
  0.0 63.6 %shard_map.55 = bf16[128,1024]{1,0:T(8,128)(2,1)} custom-call(s32[128]{0:T(128)} %docs.1, bf16[128,512]{1,0:T(8,128)(2,1)} %q_hbm.1, bf16[128,128]{1,0:T(8,128)(2,1)} %k_hbm.1, bf16[128,128]{1,0:T(8,128)(2,1)} %v_hbm.1, bf16[512,4096]{1,0:T(8,128)(2,1)} %w_hbm.1), custom_call_target="tpu_custom_call" | custom-call | tf_op jit(solution)/shard_map/pallas_call | solution.py:253
  63.6 1.7 %copy.7 = bf16[128,1024]{1,0:T(8,128)(2,1)} copy(bf16[128,1024]{1,0:T(8,128)(2,1)} %shard_map.55) | data formatting | bytes 524288

commit v2 on v1

v2 whole, which is shorter than its diff:
```python
import functools

import jax
import jax.numpy as jnp
from jax import lax
from jax.experimental import pallas as pl
from jax.experimental.pallas import tpu as pltpu
from jax.sharding import PartitionSpec as P

HD = 128
BLK = 128
GROUP = 4
EDGES = ((0, 2), (0, 14), (0, 1), (0, 15), (0, 16), (2, 4), (14, 12), (4, 6), (12, 10), (2, 3), (14, 13), (4, 5), (12, 11), (6, 7), (10, 9))
HALVES = ((6, 8, 0),)
SLOTS = (0, 16, 2, 14, 1, 15, 4, 12, 3, 13, 6, 10, 5, 11, 7, 9, 8)
CHUNKS = ((2, 14, 1, 15), (4, 12, 3, 13), (6, 10, 5, 11), (7, 9, 8))
PARTS = (0,)
COUNT = len(SLOTS)
SLOT = {chips: at for at, chips in enumerate(SLOTS)}
ROUTES = tuple((a, b, p) for a, b in EDGES for p in PARTS) + HALVES
STEPS = tuple(sorted({b - a for a, b, _ in ROUTES}))
COEF = 1.4426950408889634 / HD**0.5
FAR = 1e30
MESH = pl.DeviceIdType.MESH


def kernel(
    docs_hbm, q_hbm, k_hbm, v_hbm, w_hbm, out,
    q_in, qs, kv, wv, acc, row_max, row_sum, att,
    p_out, p_in,
    docs, loc_sem, send_sem, share_send, recv_sem, rs_send, rs_recv,
):
    s = lax.axis_index("seq")
    y = lax.axis_index("head")
    n = lax.axis_size("seq")
    heads = lax.axis_size("head")
    rows = BLK * GROUP
    width = wv.shape[2]
    half = width // 2
    reach = {step: lax.rem(s + n + 2 * step, n) for step in STEPS}
    back = {step: lax.rem(s + n - 2 * step, n) for step in STEPS if -step not in STEPS}
    mate = s + 1 - 2 * lax.rem(s, 2)
    up = lax.rem(y + 1, heads)
    down = lax.rem(y + heads - 1, heads)
    across = lax.rem(y + 2, heads)

    k_load = pltpu.make_async_copy(k_hbm, kv.at[0, 0], loc_sem.at[0])
    v_load = pltpu.make_async_copy(v_hbm, kv.at[0, 1], loc_sem.at[1])
    q_load = pltpu.make_async_copy(q_hbm, q_in, loc_sem.at[2])
    docs_load = pltpu.make_async_copy(docs_hbm, docs, loc_sem.at[7])
    docs_load.start()
    k_load.start()
    v_load.start()
    q_load.start()

    barrier = pltpu.get_barrier_semaphore()
    for peer in (*reach.values(), *back.values(), mate):
        pl.semaphore_signal(barrier, inc=1, device_id={"seq": peer}, device_id_type=MESH)
    for peer in (up, down):
        pl.semaphore_signal(barrier, inc=1, device_id={"head": peer}, device_id_type=MESH)

    w_loads = []
    for i, dest in enumerate((across, up, down, y)):
        columns = pl.ds(pl.multiple_of(dest * width, width), width)
        load = pltpu.make_async_copy(w_hbm.at[:, columns], wv.at[i], loc_sem.at[3 + i])
        load.start()
        w_loads.append(load)
    pl.semaphore_wait(barrier, len(reach) + len(back) + 3)

    def send(frm, to, part):
        buf = kv
        route = ROUTES.index((frm, to, part))
        return pltpu.make_async_remote_copy(
            src_ref=buf.at[SLOT[frm]],
            dst_ref=buf.at[SLOT[to]],
            send_sem=send_sem.at[route],
            recv_sem=recv_sem.at[SLOT[to], part],
            device_id={"seq": reach[to - frm]},
            device_id_type=MESH,
        )

    def share(chips, part):
        buf = kv
        return pltpu.make_async_remote_copy(
            src_ref=buf.at[SLOT[chips]],
            dst_ref=buf.at[COUNT + SLOT[chips]],
            send_sem=share_send.at[SLOT[chips], part],
            recv_sem=recv_sem.at[COUNT + SLOT[chips], part],
            device_id={"seq": mate},
            device_id_type=MESH,
        )

    def spread(chips, part):
        for a, b, p in ROUTES:
            if (a, p) == (chips, part):
                send(a, b, p).start()

    parent = {(b, p): a for a, b, p in ROUTES}

    def arrive(*chips):
        for c in chips:
            for part in PARTS:
                send(parent[c, part], c, part).wait_recv()
                spread(c, part)
            for part in PARTS:
                share(c, part).start()

    def shared(*chips):
        for c in chips:
            for part in PARTS:
                share(c, part).wait_recv()

    def penalty(distance):
        other = s - distance
        same = docs[jnp.maximum(other, 0)] == docs[s]
        return jnp.where(same & (other >= 0) & (distance > 0), 0.0, FAR).astype(jnp.float32)

    def absorb(first, count, penalties):
        keys = kv[first:first + count, 0].reshape(count * BLK, HD)
        values = kv[first:first + count, 1].reshape(count * BLK, HD)
        scores = lax.dot_general(
            keys, qs[...], (((1,), (1,)), ((), ())), preferred_element_type=jnp.float32
        )
        parts = [scores[i * BLK:(i + 1) * BLK] for i in range(count)]
        old = row_max[...]
        new = old
        for part, pen in zip(parts, penalties):
            new = jnp.maximum(new, jnp.max(part, axis=0, keepdims=True) - pen)
        factor = jnp.exp2((old - new) * COEF)
        total = row_sum[...] * factor
        weights = []
        for part, pen in zip(parts, penalties):
            weight = jnp.exp2((part - (new + pen)) * COEF)
            total = total + jnp.sum(weight, axis=0, keepdims=True)
            weights.append(weight.astype(jnp.bfloat16))
        product = lax.dot_general(
            values, jnp.concatenate(weights, axis=0), (((0,), (0,)), ((), ())),
            preferred_element_type=jnp.float32,
        )
        acc[...] = acc[...] * factor + product
        row_max[...] = new
        row_sum[...] = total

    k_load.wait()
    v_load.wait()
    spread(0, 0)
    for part in PARTS:
        share(0, part).start()

    docs_load.wait()
    q_load.wait()
    for g in range(GROUP):
        qs[g * BLK:(g + 1) * BLK, :] = q_in[:, g * HD:(g + 1) * HD]

    scores = lax.dot_general(
        kv[0, 0], qs[...], (((1,), (1,)), ((), ())), preferred_element_type=jnp.float32
    )
    key_at = lax.broadcasted_iota(jnp.int32, (BLK, rows), 0)
    query_at = lax.rem(lax.broadcasted_iota(jnp.int32, (BLK, rows), 1), BLK)
    scores = jnp.where(key_at <= query_at, scores, -FAR)
    top = jnp.max(scores, axis=0, keepdims=True)
    weight = jnp.exp2((scores - top) * COEF)
    row_max[...] = top
    row_sum[...] = jnp.sum(weight, axis=0, keepdims=True)
    acc[...] = lax.dot_general(
        kv[0, 1], weight.astype(jnp.bfloat16), (((0,), (0,)), ((), ())),
        preferred_element_type=jnp.float32,
    )

    skew = 2 * lax.rem(s, 2) - 1

    def mine(chips):
        absorb(SLOT[chips[0]], len(chips), [penalty(2 * c) for c in chips])

    def other(chips):
        shared(*chips)
        absorb(COUNT + SLOT[chips[0]], len(chips), [penalty(2 * c + skew) for c in chips])

    arrive(*CHUNKS[0], 16)
    mine(CHUNKS[0])
    arrive(*CHUNKS[1])
    other((0, 16))
    other(CHUNKS[0])
    mine(CHUNKS[1])
    arrive(*CHUNKS[2])
    other(CHUNKS[1])
    mine(CHUNKS[2])
    arrive(*CHUNKS[3])
    mine(CHUNKS[3])
    other(CHUNKS[2])
    other(CHUNKS[3])

    scaled = acc[...] / row_sum[...]
    for g in range(GROUP):
        att[:, g * HD:(g + 1) * HD] = scaled[:, g * BLK:(g + 1) * BLK].T.astype(jnp.bfloat16)

    def project(i, side):
        return jnp.dot(
            att[...], wv[i, :, side * half:(side + 1) * half],
            preferred_element_type=jnp.float32,
        )

    def give(stage, side):
        return pltpu.make_async_remote_copy(
            src_ref=p_out.at[stage, side],
            dst_ref=p_in.at[stage, side],
            send_sem=rs_send.at[stage, side],
            recv_sem=rs_recv.at[stage, side],
            device_id={"head": up if side == 0 else down},
            device_id_type=MESH,
        )

    w_loads[0].wait()
    for side in (0, 1):
        p_out[0, side] = project(0, side).astype(jnp.bfloat16)
        give(0, side).start()
    w_loads[1].wait()
    w_loads[2].wait()
    for side in (0, 1):
        p_out[1, side] = project(1 + side, 1 - side).astype(jnp.bfloat16)
        give(1, side).start()
    held = [project(1 + side, side) for side in (0, 1)]
    for side in (0, 1):
        give(0, side).wait_recv()
        p_out[2, side] = (held[side] + p_in[0, side].astype(jnp.float32)).astype(jnp.bfloat16)
        give(2, side).start()
    w_loads[3].wait()
    own = [project(3, side) for side in (0, 1)]
    for side in (0, 1):
        give(1, 1 - side).wait_recv()
        own[side] = own[side] + p_in[1, 1 - side].astype(jnp.float32)
    for side in (0, 1):
        give(2, side).wait_recv()
        out[:, side * half:(side + 1) * half] = (
            own[side] + p_in[2, side].astype(jnp.float32)
        ).astype(jnp.bfloat16)

    for route in ROUTES:
        send(*route).wait_send()
    for chips in SLOTS:
        for part in PARTS:
            share(chips, part).wait_send()
    for stage in (0, 1, 2):
        for side in (0, 1):
            give(stage, side).wait_send()


def local(query_states, key_states, value_states, out_weight, block_docs):
    query_states, key_states, value_states, out_weight, block_docs = [pltpu.with_memory_space_constraint(a, pltpu.HBM) for a in (query_states, key_states, value_states, out_weight, block_docs)]
    tokens = query_states.shape[0]
    model = out_weight.shape[1]
    width = model // lax.axis_size("head")
    rows = GROUP * BLK
    any_space = pl.BlockSpec(memory_space=pltpu.HBM)
    return pl.pallas_call(
        kernel,
        out_shape=jax.ShapeDtypeStruct((tokens, width), jnp.bfloat16),
        in_specs=[any_space] * 5,
        out_specs=pl.BlockSpec(memory_space=pltpu.VMEM),
        scratch_shapes=[
            pltpu.VMEM((tokens, rows), jnp.bfloat16),
            pltpu.VMEM((rows, HD), jnp.bfloat16),
            pltpu.VMEM((2 * COUNT, 2, BLK, HD), jnp.bfloat16),
            pltpu.VMEM((4, rows, width), jnp.bfloat16),
            pltpu.VMEM((HD, rows), jnp.float32),
            pltpu.VMEM((1, rows), jnp.float32),
            pltpu.VMEM((1, rows), jnp.float32),
            pltpu.VMEM((tokens, rows), jnp.bfloat16),
            pltpu.VMEM((3, 2, tokens, width // 2), jnp.bfloat16),
            pltpu.VMEM((3, 2, tokens, width // 2), jnp.bfloat16),
            pltpu.SMEM((128,), jnp.int32),
            pltpu.SemaphoreType.DMA((8,)),
            pltpu.SemaphoreType.DMA((len(ROUTES),)),
            pltpu.SemaphoreType.DMA((COUNT, 2)),
            pltpu.SemaphoreType.DMA((2 * COUNT, 2)),
            pltpu.SemaphoreType.DMA((3, 2)),
            pltpu.SemaphoreType.DMA((3, 2)),
        ],
        compiler_params=pltpu.CompilerParams(
            collective_id=0, has_side_effects=True, vmem_limit_bytes=20 << 20
        ),
    )(block_docs, query_states, key_states, value_states, out_weight)


def solution(mesh):
    return jax.shard_map(
        local,
        mesh=mesh,
        in_specs=(P("seq", "head"), P("seq", "head"), P("seq", "head"), P("head", None), P()),
        out_specs=P("seq", "head"),
        check_vma=False,
    )
```

time: 65.4 us -> 49.8 us (0.76)
  Pallas kernels: 63.6 us -> 48.9 us
  local copies, waits for them, and re-layouts: 1.67 us -> 0.71 us
    pallas_call x1, Pallas kernels: 63.6 us -> 48.9 us  [local(): pl.pallas_call(kernel, out_shape=jax.ShapeDtypeStruct((tokens, width), jn...]
    unnamed x1, local copies, waits for them, and re-layouts: 1.67 us -> 0.71 us
where the time goes in v2:
time: 49.8 us; the launch traced here: 49.7 us
  Pallas kernels  48.9 us (98%)
  local copies, waits for them, and re-layouts  0.71 us (1%)
    pallas_call x1, Pallas kernels, local(): pl.pallas_call(kernel, out_shape=jax.ShapeDtypeStruct((tokens, width), jn...  48.9 us

profile of v2, /device:TPU:1, one launch (start us, length us, event | category | flops | bytes accessed | tf_op | source)
XLA Modules:
  0.0 49.7 jit_solution(11178780130057395228)
XLA Ops:
  0.0 48.9 %shard_map.55 = bf16[128,1024]{1,0:T(8,128)(2,1)S(1)} custom-call(s32[128]{0:T(128)} %docs_hbm.1, bf16[128,512]{1,0:T(8,128)(2,1)} %q_hbm.1, bf16[128,128]{1,0:T(8,128)(2,1)} %k_hbm.1, bf16[128,128]{1,0:T(8,128)(2,1)} %v_hbm.1, bf16[512,4096]{1,0:T(8,128)(2,1)} %w_hbm.1), custom_call_target="tpu_custom_call" | custom-call | tf_op jit(solution)/shard_map/pallas_call | solution.py:255
  49.0 0.7 %copy.7 = bf16[128,1024]{1,0:T(8,128)(2,1)} copy(bf16[128,1024]{1,0:T(8,128)(2,1)S(1)} %shard_map.55) | data formatting | bytes 524288

commit v3 on v2

v3 whole, which is shorter than its diff:
```python
import functools

import jax
import jax.numpy as jnp
from jax import lax
from jax.experimental import pallas as pl
from jax.experimental.pallas import tpu as pltpu
from jax.sharding import PartitionSpec as P

HD = 128
BLK = 128
GROUP = 4
CHAIN = ((0, 2), (0, 14), (2, 4), (14, 12), (4, 6), (12, 10))
LEAVES = (
    (0, 1), (0, 15), (0, 16),
    (2, 3), (14, 13), (4, 5), (12, 11), (6, 7), (10, 9),
)
LAST = ((6, 8, 0), (10, 8, 1))
SLOTS = (0, 16, 2, 14, 1, 15, 4, 12, 3, 13, 6, 10, 5, 11, 7, 9, 8)
OWN, UP, DOWN, ACROSS = range(4)
CHUNKS = ((2, 14, 1, 15), (4, 12, 3, 13), (6, 10, 5, 11), (7, 9, 8))
COUNT = len(SLOTS)
SLOT = {chips: at for at, chips in enumerate(SLOTS)}
ROUTES = tuple((a, b, p) for a, b in CHAIN for p in (0, 1)) + LAST + tuple((a, b, 2) for a, b in LEAVES)
PARENT = {(b, p): a for a, b, p in ROUTES}
STEPS = tuple(sorted({b - a for a, b, _ in ROUTES}))
COEF = 1.4426950408889634 / HD**0.5
FAR = 1e30
MESH = pl.DeviceIdType.MESH


def kernel(
    docs_hbm, q_hbm, k_hbm, v_hbm, w_hbm, out,
    q_in, qs, kv, wx, transit, acc, row_max, row_sum, att, ax, mixed,
    docs, loc_sem, send_sem, share_send, recv_sem, share_recv, w_send, w_recv, a_send, a_recv,
):
    s = lax.axis_index("seq")
    y = lax.axis_index("head")
    n = lax.axis_size("seq")
    heads = lax.axis_size("head")
    rows = BLK * GROUP
    width = wx.shape[2]
    side_rows = rows // 2
    quarter = rows // 4
    token_half = BLK // 2
    reach = {step: lax.rem(s + n + 2 * step, n) for step in STEPS}
    back = {step: lax.rem(s + n - 2 * step, n) for step in STEPS if -step not in STEPS}
    mate = s + 1 - 2 * lax.rem(s, 2)
    up = lax.rem(y + 1, heads)
    down = lax.rem(y + heads - 1, heads)
    across = lax.rem(y + 2, heads)

    k_load = pltpu.make_async_copy(k_hbm, kv.at[0, 0], loc_sem.at[0])
    v_load = pltpu.make_async_copy(v_hbm, kv.at[0, 1], loc_sem.at[1])
    q_load = pltpu.make_async_copy(q_hbm, q_in, loc_sem.at[2])
    docs_load = pltpu.make_async_copy(docs_hbm, docs, loc_sem.at[4])
    docs_load.start()
    k_load.start()
    v_load.start()
    q_load.start()

    barrier = pltpu.get_barrier_semaphore()
    for peer in (*reach.values(), *back.values(), mate):
        pl.semaphore_signal(barrier, inc=1, device_id={"seq": peer}, device_id_type=MESH)
    for peer in (up, down):
        pl.semaphore_signal(barrier, inc=1, device_id={"head": peer}, device_id_type=MESH)

    def columns(dest):
        return pl.ds(pl.multiple_of(dest * width, width), width)

    w_own = pltpu.make_async_copy(w_hbm.at[:, columns(y)], wx.at[OWN], loc_sem.at[3])
    w_own.start()
    pl.semaphore_wait(barrier, len(reach) + len(back) + 3)

    def view(slot, part):
        return kv.at[slot] if part == 2 else kv.at[slot, part]

    def send(frm, to, part):
        route = ROUTES.index((frm, to, part))
        return pltpu.make_async_remote_copy(
            src_ref=view(SLOT[frm], part),
            dst_ref=view(SLOT[to], part),
            send_sem=send_sem.at[route],
            recv_sem=recv_sem.at[SLOT[to], part],
            device_id={"seq": reach[to - frm]},
            device_id_type=MESH,
        )

    def share(chips):
        return pltpu.make_async_remote_copy(
            src_ref=kv.at[SLOT[chips]],
            dst_ref=kv.at[COUNT + SLOT[chips]],
            send_sem=share_send.at[SLOT[chips]],
            recv_sem=share_recv.at[SLOT[chips]],
            device_id={"seq": mate},
            device_id_type=MESH,
        )

    def spread(chips, part):
        for a, b, p in ROUTES:
            if (a, p) == (chips, part):
                send(a, b, p).start()

    def arrive(*chips):
        for c in chips:
            for part in (0, 1, 2):
                if (c, part) in PARENT:
                    send(PARENT[c, part], c, part).wait_recv()
                    if part < 2:
                        spread(c, part)
            spread(c, 2)
            share(c).start()

    def shared(*chips):
        for c in chips:
            share(c).wait_recv()

    first_row = pl.multiple_of(lax.rem(s, 2) * side_rows, side_rows)

    def over(side, src, dst, at):
        return pltpu.make_async_remote_copy(
            src_ref=src, dst_ref=dst, send_sem=w_send.at[at], recv_sem=w_recv.at[at],
            device_id={"head": up if side == 0 else down}, device_id_type=MESH,
        )

    def w_first(side):
        span = pl.ds(first_row + side * quarter, quarter)
        return over(side, w_hbm.at[span, columns(across)], transit.at[side], side)

    def w_direct(side):
        span = pl.ds(first_row, side_rows)
        dest = up if side == 0 else down
        return over(side, w_hbm.at[span, columns(dest)], wx.at[DOWN - side, span], 2 + side)

    def w_onward(side):
        span = pl.ds(first_row + side * quarter, quarter)
        return over(side, transit.at[side], wx.at[ACROSS, span], 4 + side)

    def w_share(group):
        span = pl.ds(first_row, side_rows)
        return pltpu.make_async_remote_copy(
            src_ref=wx.at[group, span], dst_ref=wx.at[group, span],
            send_sem=w_send.at[5 + group], recv_sem=w_recv.at[5 + group],
            device_id={"seq": mate}, device_id_type=MESH,
        )

    def penalty(distance):
        other = s - distance
        same = docs[jnp.maximum(other, 0)] == docs[s]
        return jnp.where(same & (other >= 0) & (distance > 0), 0.0, FAR).astype(jnp.float32)

    def absorb(first, count, penalties):
        keys = kv[first:first + count, 0].reshape(count * BLK, HD)
        values = kv[first:first + count, 1].reshape(count * BLK, HD)
        scores = lax.dot_general(
            keys, qs[...], (((1,), (1,)), ((), ())), preferred_element_type=jnp.float32
        )
        parts = [scores[i * BLK:(i + 1) * BLK] for i in range(count)]
        old = row_max[...]
        new = old
        for part, pen in zip(parts, penalties):
            new = jnp.maximum(new, jnp.max(part, axis=0, keepdims=True) - pen)
        factor = jnp.exp2((old - new) * COEF)
        total = row_sum[...] * factor
        weights = []
        for part, pen in zip(parts, penalties):
            weight = jnp.exp2((part - (new + pen)) * COEF)
            total = total + jnp.sum(weight, axis=0, keepdims=True)
            weights.append(weight.astype(jnp.bfloat16))
        product = lax.dot_general(
            values, jnp.concatenate(weights, axis=0), (((0,), (0,)), ((), ())),
            preferred_element_type=jnp.float32,
        )
        acc[...] = acc[...] * factor + product
        row_max[...] = new
        row_sum[...] = total

    k_load.wait()
    spread(0, 0)
    v_load.wait()
    spread(0, 1)
    spread(0, 2)
    share(0).start()
    for side in (0, 1):
        w_first(side).start()
    for side in (0, 1):
        w_direct(side).start()

    docs_load.wait()
    q_load.wait()
    for g in range(GROUP):
        qs[g * BLK:(g + 1) * BLK, :] = q_in[:, g * HD:(g + 1) * HD]

    scores = lax.dot_general(
        kv[0, 0], qs[...], (((1,), (1,)), ((), ())), preferred_element_type=jnp.float32
    )
    key_at = lax.broadcasted_iota(jnp.int32, (BLK, rows), 0)
    query_at = lax.rem(lax.broadcasted_iota(jnp.int32, (BLK, rows), 1), BLK)
    scores = jnp.where(key_at <= query_at, scores, -FAR)
    top = jnp.max(scores, axis=0, keepdims=True)
    weight = jnp.exp2((scores - top) * COEF)
    row_max[...] = top
    row_sum[...] = jnp.sum(weight, axis=0, keepdims=True)
    acc[...] = lax.dot_general(
        kv[0, 1], weight.astype(jnp.bfloat16), (((0,), (0,)), ((), ())),
        preferred_element_type=jnp.float32,
    )

    skew = 2 * lax.rem(s, 2) - 1

    def mine(chips):
        absorb(SLOT[chips[0]], len(chips), [penalty(2 * c) for c in chips])

    def other(chips):
        shared(*chips)
        absorb(COUNT + SLOT[chips[0]], len(chips), [penalty(2 * c + skew) for c in chips])

    arrive(*CHUNKS[0], 16)
    mine(CHUNKS[0])
    arrive(*CHUNKS[1])
    for side in (0, 1):
        w_first(side).wait_recv()
        w_onward(side).start()
    other((0, 16))
    other(CHUNKS[0])
    mine(CHUNKS[1])
    arrive(*CHUNKS[2])
    other(CHUNKS[1])
    mine(CHUNKS[2])
    arrive(*CHUNKS[3])
    mine(CHUNKS[3])
    other(CHUNKS[2])
    for side in (0, 1):
        w_direct(side).wait_recv()
        w_share(DOWN - side).start()
    other(CHUNKS[3])

    scaled = acc[...] / row_sum[...]
    for g in range(GROUP):
        att[:, g * HD:(g + 1) * HD] = scaled[:, g * BLK:(g + 1) * BLK].T.astype(jnp.bfloat16)

    def a_give(side, piece):
        span = pl.ds(piece * token_half, token_half)
        return pltpu.make_async_remote_copy(
            src_ref=att.at[span], dst_ref=ax.at[1 - side, span],
            send_sem=a_send.at[side, piece], recv_sem=a_recv.at[side, piece],
            device_id={"head": up if side == 0 else down}, device_id_type=MESH,
        )

    def a_onward(side):
        span = pl.ds(side * token_half, token_half)
        return pltpu.make_async_remote_copy(
            src_ref=ax.at[1 - side, span], dst_ref=ax.at[2, span],
            send_sem=a_send.at[side, 2], recv_sem=a_recv.at[side, 2],
            device_id={"head": up if side == 0 else down}, device_id_type=MESH,
        )

    for side, piece in ((0, 0), (1, 1), (0, 1), (1, 0)):
        a_give(side, piece).start()
    w_own.wait()
    mixed[...] = jnp.dot(att[...], wx[OWN], preferred_element_type=jnp.float32)
    for side in (0, 1):
        a_give(side, side).wait_recv()
        a_onward(side).start()
    for side in (0, 1):
        w_onward(side).wait_recv()
    w_share(ACROSS).start()
    for side in (0, 1):
        a_give(side, 1 - side).wait_recv()
        w_share(DOWN - side).wait_recv()
        mixed[...] += jnp.dot(ax[1 - side], wx[DOWN - side], preferred_element_type=jnp.float32)
    w_share(ACROSS).wait_recv()
    for side in (0, 1):
        a_onward(side).wait_recv()
    out[...] = (
        mixed[...] + jnp.dot(ax[2], wx[ACROSS], preferred_element_type=jnp.float32)
    ).astype(jnp.bfloat16)

    for route in ROUTES:
        send(*route).wait_send()
    for chips in SLOTS:
        share(chips).wait_send()
    for side in (0, 1):
        w_first(side).wait_send()
        w_direct(side).wait_send()
        w_onward(side).wait_send()
        for piece in (0, 1):
            a_give(side, piece).wait_send()
        a_onward(side).wait_send()
    for group in (UP, DOWN, ACROSS):
        w_share(group).wait_send()


def local(query_states, key_states, value_states, out_weight, block_docs):
    query_states, key_states, value_states, out_weight, block_docs = [pltpu.with_memory_space_constraint(a, pltpu.HBM) for a in (query_states, key_states, value_states, out_weight, block_docs)]
    tokens = query_states.shape[0]
    model = out_weight.shape[1]
    width = model // lax.axis_size("head")
    rows = GROUP * BLK
    any_space = pl.BlockSpec(memory_space=pltpu.HBM)
    return pl.pallas_call(
        kernel,
        out_shape=jax.ShapeDtypeStruct((tokens, width), jnp.bfloat16),
        in_specs=[any_space] * 5,
        out_specs=pl.BlockSpec(memory_space=pltpu.VMEM),
        scratch_shapes=[
            pltpu.VMEM((tokens, rows), jnp.bfloat16),
            pltpu.VMEM((rows, HD), jnp.bfloat16),
            pltpu.VMEM((2 * COUNT, 2, BLK, HD), jnp.bfloat16),
            pltpu.VMEM((4, rows, width), jnp.bfloat16),
            pltpu.VMEM((2, rows // 4, width), jnp.bfloat16),
            pltpu.VMEM((HD, rows), jnp.float32),
            pltpu.VMEM((1, rows), jnp.float32),
            pltpu.VMEM((1, rows), jnp.float32),
            pltpu.VMEM((tokens, rows), jnp.bfloat16),
            pltpu.VMEM((3, tokens, rows), jnp.bfloat16),
            pltpu.VMEM((tokens, width), jnp.float32),
            pltpu.SMEM((128,), jnp.int32),
            pltpu.SemaphoreType.DMA((5,)),
            pltpu.SemaphoreType.DMA((len(ROUTES),)),
            pltpu.SemaphoreType.DMA((COUNT,)),
            pltpu.SemaphoreType.DMA((COUNT, 3)),
            pltpu.SemaphoreType.DMA((COUNT,)),
            pltpu.SemaphoreType.DMA((9,)),
            pltpu.SemaphoreType.DMA((9,)),
            pltpu.SemaphoreType.DMA((2, 3)),
            pltpu.SemaphoreType.DMA((2, 3)),
        ],
        compiler_params=pltpu.CompilerParams(
            collective_id=0, has_side_effects=True, vmem_limit_bytes=20 << 20
        ),
    )(block_docs, query_states, key_states, value_states, out_weight)


def solution(mesh):
    return jax.shard_map(
        local,
        mesh=mesh,
        in_specs=(P("seq", "head"), P("seq", "head"), P("seq", "head"), P("head", None), P()),
        out_specs=P("seq", "head"),
        check_vma=False,
    )
```

time: 49.8 us -> 46.6 us (0.936)
  Pallas kernels: 48.9 us -> 45.8 us
    pallas_call x1, Pallas kernels: 48.9 us -> 45.8 us  [local(): pl.pallas_call(kernel, out_shape=jax.ShapeDtypeStruct((tokens, width), jn...]
where the time goes in v3:
time: 46.6 us; the launch traced here: 46.5 us
  Pallas kernels  45.8 us (98%)
  local copies, waits for them, and re-layouts  0.71 us (2%)
    pallas_call x1, Pallas kernels, local(): pl.pallas_call(kernel, out_shape=jax.ShapeDtypeStruct((tokens, width), jn...  45.8 us

profile of v3, /device:TPU:1, one launch (start us, length us, event | category | flops | bytes accessed | tf_op | source)
XLA Modules:
  0.0 46.5 jit_solution(9546540903711423507)
XLA Ops:
  0.0 45.8 %shard_map.55 = bf16[128,1024]{1,0:T(8,128)(2,1)S(1)} custom-call(s32[128]{0:T(128)} %docs_hbm.1, bf16[128,512]{1,0:T(8,128)(2,1)} %q_hbm.1, bf16[128,128]{1,0:T(8,128)(2,1)} %k_hbm.1, bf16[128,128]{1,0:T(8,128)(2,1)} %v_hbm.1, bf16[512,4096]{1,0:T(8,128)(2,1)} %w_hbm.1), custom_call_target="tpu_custom_call" | custom-call | tf_op jit(solution)/shard_map/pallas_call | solution.py:301
  45.8 0.7 %copy.7 = bf16[128,1024]{1,0:T(8,128)(2,1)} copy(bf16[128,1024]{1,0:T(8,128)(2,1)S(1)} %shard_map.55) | data formatting | bytes 524288

commit v4 on v3

--- a/solution.py
+++ b/solution.py
@@ -21,7 +21,9 @@
 CHUNKS = ((2, 14, 1, 15), (4, 12, 3, 13), (6, 10, 5, 11), (7, 9, 8))
 COUNT = len(SLOTS)
 SLOT = {chips: at for at, chips in enumerate(SLOTS)}
-ROUTES = tuple((a, b, p) for a, b in CHAIN for p in (0, 1)) + LAST + tuple((a, b, 2) for a, b in LEAVES)
+PARTS = (0, 1)
+WHOLE = 2
+ROUTES = tuple((a, b, p) for a, b in CHAIN for p in PARTS) + LAST + tuple((a, b, WHOLE) for a, b in LEAVES)
 PARENT = {(b, p): a for a, b, p in ROUTES}
 STEPS = tuple(sorted({b - a for a, b, _ in ROUTES}))
 COEF = 1.4426950408889634 / HD**0.5
@@ -73,7 +75,7 @@
     pl.semaphore_wait(barrier, len(reach) + len(back) + 3)
 
     def view(slot, part):
-        return kv.at[slot] if part == 2 else kv.at[slot, part]
+        return kv.at[slot] if part == WHOLE else kv.at[slot, part]
 
     def send(frm, to, part):
         route = ROUTES.index((frm, to, part))
@@ -102,13 +104,15 @@
                 send(a, b, p).start()
 
     def arrive(*chips):
-        for c in chips:
-            for part in (0, 1, 2):
+        for part in PARTS:
+            for c in chips:
                 if (c, part) in PARENT:
                     send(PARENT[c, part], c, part).wait_recv()
-                    if part < 2:
-                        spread(c, part)
-            spread(c, 2)
+                    spread(c, part)
+        for c in chips:
+            if (c, WHOLE) in PARENT:
+                send(PARENT[c, WHOLE], c, WHOLE).wait_recv()
+            spread(c, WHOLE)
             share(c).start()
 
     def shared(*chips):
@@ -179,7 +183,7 @@
     spread(0, 0)
     v_load.wait()
     spread(0, 1)
-    spread(0, 2)
+    spread(0, WHOLE)
     share(0).start()
     for side in (0, 1):
         w_first(side).start()
@@ -227,9 +231,9 @@
     arrive(*CHUNKS[2])
     other(CHUNKS[1])
     mine(CHUNKS[2])
+    other(CHUNKS[2])
     arrive(*CHUNKS[3])
     mine(CHUNKS[3])
-    other(CHUNKS[2])
     for side in (0, 1):
         w_direct(side).wait_recv()
         w_share(DOWN - side).start()
@@ -265,6 +269,17 @@
     for side in (0, 1):
         w_onward(side).wait_recv()
     w_share(ACROSS).start()
+    for route in ROUTES:
+        send(*route).wait_send()
+    for chips in SLOTS:
+        share(chips).wait_send()
+    for side in (0, 1):
+        w_first(side).wait_send()
+        w_direct(side).wait_send()
+        w_onward(side).wait_send()
+        w_share(DOWN - side).wait_send()
+        for piece in (0, 1):
+            a_give(side, piece).wait_send()
     for side in (0, 1):
         a_give(side, 1 - side).wait_recv()
         w_share(DOWN - side).wait_recv()
@@ -276,19 +291,9 @@
         mixed[...] + jnp.dot(ax[2], wx[ACROSS], preferred_element_type=jnp.float32)
     ).astype(jnp.bfloat16)
 
-    for route in ROUTES:
-        send(*route).wait_send()
-    for chips in SLOTS:
-        share(chips).wait_send()
-    for side in (0, 1):
-        w_first(side).wait_send()
-        w_direct(side).wait_send()
-        w_onward(side).wait_send()
-        for piece in (0, 1):
-            a_give(side, piece).wait_send()
+    w_share(ACROSS).wait_send()
+    for side in (0, 1):
         a_onward(side).wait_send()
-    for group in (UP, DOWN, ACROSS):
-        w_share(group).wait_send()
 
 
 def local(query_states, key_states, value_states, out_weight, block_docs):

time: 46.6 us -> 46.1 us (0.989)
  Pallas kernels: 45.8 us -> 45.3 us
    pallas_call x1, Pallas kernels: 45.8 us -> 45.3 us  [local(): pl.pallas_call(kernel, out_shape=jax.ShapeDtypeStruct((tokens, width), jn...]
where the time goes in v4:
time: 46.1 us; the launch traced here: 46 us
  Pallas kernels  45.3 us (98%)
  local copies, waits for them, and re-layouts  0.71 us (2%)
    pallas_call x1, Pallas kernels, local(): pl.pallas_call(kernel, out_shape=jax.ShapeDtypeStruct((tokens, width), jn...  45.3 us

profile of v4, /device:TPU:1, one launch (start us, length us, event | category | flops | bytes accessed | tf_op | source)
XLA Modules:
  0.0 46.0 jit_solution(87371906427748221)
XLA Ops:
  0.0 45.3 %shard_map.55 = bf16[128,1024]{1,0:T(8,128)(2,1)S(1)} custom-call(s32[128]{0:T(128)} %docs_hbm.1, bf16[128,512]{1,0:T(8,128)(2,1)} %q_hbm.1, bf16[128,128]{1,0:T(8,128)(2,1)} %k_hbm.1, bf16[128,128]{1,0:T(8,128)(2,1)} %v_hbm.1, bf16[512,4096]{1,0:T(8,128)(2,1)} %w_hbm.1), custom_call_target="tpu_custom_call" | custom-call | tf_op jit(solution)/shard_map/pallas_call | solution.py:306
  45.3 0.7 %copy.7 = bf16[128,1024]{1,0:T(8,128)(2,1)} copy(bf16[128,1024]{1,0:T(8,128)(2,1)S(1)} %shard_map.55) | data formatting | bytes 524288

commit v5 on v4

--- a/solution.py
+++ b/solution.py
@@ -52,6 +52,12 @@
     down = lax.rem(y + heads - 1, heads)
     across = lax.rem(y + 2, heads)
 
+    barrier = pltpu.get_barrier_semaphore()
+    for peer in (*reach.values(), *back.values(), mate):
+        pl.semaphore_signal(barrier, inc=1, device_id={"seq": peer}, device_id_type=MESH)
+    for peer in (up, down):
+        pl.semaphore_signal(barrier, inc=1, device_id={"head": peer}, device_id_type=MESH)
+
     k_load = pltpu.make_async_copy(k_hbm, kv.at[0, 0], loc_sem.at[0])
     v_load = pltpu.make_async_copy(v_hbm, kv.at[0, 1], loc_sem.at[1])
     q_load = pltpu.make_async_copy(q_hbm, q_in, loc_sem.at[2])
@@ -61,12 +67,6 @@
     v_load.start()
     q_load.start()
 
-    barrier = pltpu.get_barrier_semaphore()
-    for peer in (*reach.values(), *back.values(), mate):
-        pl.semaphore_signal(barrier, inc=1, device_id={"seq": peer}, device_id_type=MESH)
-    for peer in (up, down):
-        pl.semaphore_signal(barrier, inc=1, device_id={"head": peer}, device_id_type=MESH)
-
     def columns(dest):
         return pl.ds(pl.multiple_of(dest * width, width), width)
 
@@ -80,7 +80,7 @@
     def send(frm, to, part):
         route = ROUTES.index((frm, to, part))
         return pltpu.make_async_remote_copy(
-            src_ref=view(SLOT[frm], part),
+            src_ref=(k_hbm, v_hbm)[part] if frm == 0 and part < WHOLE else view(SLOT[frm], part),
             dst_ref=view(SLOT[to], part),
             send_sem=send_sem.at[route],
             recv_sem=recv_sem.at[SLOT[to], part],
@@ -179,10 +179,10 @@
         row_max[...] = new
         row_sum[...] = total
 
+    spread(0, 0)
+    spread(0, 1)
     k_load.wait()
-    spread(0, 0)
     v_load.wait()
-    spread(0, 1)
     spread(0, WHOLE)
     share(0).start()
     for side in (0, 1):

time: 46.1 us -> 45.9 us (level)
  no operation moved by 1% of the time
where the time goes in v5:
time: 45.9 us; the launch traced here: 45.8 us
  Pallas kernels  45.1 us (98%)
  local copies, waits for them, and re-layouts  0.71 us (2%)
    pallas_call x1, Pallas kernels, local(): pl.pallas_call(kernel, out_shape=jax.ShapeDtypeStruct((tokens, width), jn...  45.1 us

profile of v5, /device:TPU:1, one launch (start us, length us, event | category | flops | bytes accessed | tf_op | source)
XLA Modules:
  0.0 45.8 jit_solution(13181270597941208198)
XLA Ops:
  0.0 45.1 %shard_map.55 = bf16[128,1024]{1,0:T(8,128)(2,1)S(1)} custom-call(s32[128]{0:T(128)} %docs_hbm.1, bf16[128,512]{1,0:T(8,128)(2,1)} %q_hbm.1, bf16[128,128]{1,0:T(8,128)(2,1)} %k_hbm.1, bf16[128,128]{1,0:T(8,128)(2,1)} %v_hbm.1, bf16[512,4096]{1,0:T(8,128)(2,1)} %w_hbm.1), custom_call_target="tpu_custom_call" | custom-call | tf_op jit(solution)/shard_map/pallas_call | solution.py:306
  45.1 0.7 %copy.7 = bf16[128,1024]{1,0:T(8,128)(2,1)} copy(bf16[128,1024]{1,0:T(8,128)(2,1)S(1)} %shard_map.55) | data formatting | bytes 524288

commit v6 on v4

--- a/solution.py
+++ b/solution.py
@@ -45,6 +45,7 @@
     side_rows = rows // 2
     quarter = rows // 4
     token_half = BLK // 2
+    token_part = BLK // 4
     reach = {step: lax.rem(s + n + 2 * step, n) for step in STEPS}
     back = {step: lax.rem(s + n - 2 * step, n) for step in STEPS if -step not in STEPS}
     mate = s + 1 - 2 * lax.rem(s, 2)
@@ -244,28 +245,33 @@
         att[:, g * HD:(g + 1) * HD] = scaled[:, g * BLK:(g + 1) * BLK].T.astype(jnp.bfloat16)
 
     def a_give(side, piece):
-        span = pl.ds(piece * token_half, token_half)
+        span = pl.ds(piece * token_part, token_part)
         return pltpu.make_async_remote_copy(
             src_ref=att.at[span], dst_ref=ax.at[1 - side, span],
             send_sem=a_send.at[side, piece], recv_sem=a_recv.at[side, piece],
             device_id={"head": up if side == 0 else down}, device_id_type=MESH,
         )
 
-    def a_onward(side):
-        span = pl.ds(side * token_half, token_half)
+    def a_onward(side, piece):
+        span = pl.ds((2 * side + piece) * token_part, token_part)
         return pltpu.make_async_remote_copy(
             src_ref=ax.at[1 - side, span], dst_ref=ax.at[2, span],
-            send_sem=a_send.at[side, 2], recv_sem=a_recv.at[side, 2],
+            send_sem=a_send.at[side, 4 + piece], recv_sem=a_recv.at[side, 4 + piece],
             device_id={"head": up if side == 0 else down}, device_id_type=MESH,
         )
 
-    for side, piece in ((0, 0), (1, 1), (0, 1), (1, 0)):
-        a_give(side, piece).start()
+    for piece in (0, 1):
+        for side in (0, 1):
+            a_give(side, 2 * side + piece).start()
+    for piece in (0, 1):
+        for side in (0, 1):
+            a_give(side, 2 - 2 * side + piece).start()
     w_own.wait()
     mixed[...] = jnp.dot(att[...], wx[OWN], preferred_element_type=jnp.float32)
-    for side in (0, 1):
-        a_give(side, side).wait_recv()
-        a_onward(side).start()
+    for piece in (0, 1):
+        for side in (0, 1):
+            a_give(side, 2 * side + piece).wait_recv()
+            a_onward(side, piece).start()
     for side in (0, 1):
         w_onward(side).wait_recv()
     w_share(ACROSS).start()
@@ -278,22 +284,25 @@
         w_direct(side).wait_send()
         w_onward(side).wait_send()
         w_share(DOWN - side).wait_send()
+        for piece in range(4):
+            a_give(side, piece).wait_send()
+    for side in (0, 1):
         for piece in (0, 1):
-            a_give(side, piece).wait_send()
-    for side in (0, 1):
-        a_give(side, 1 - side).wait_recv()
+            a_give(side, 2 - 2 * side + piece).wait_recv()
         w_share(DOWN - side).wait_recv()
         mixed[...] += jnp.dot(ax[1 - side], wx[DOWN - side], preferred_element_type=jnp.float32)
     w_share(ACROSS).wait_recv()
     for side in (0, 1):
-        a_onward(side).wait_recv()
+        for piece in (0, 1):
+            a_onward(side, piece).wait_recv()
     out[...] = (
         mixed[...] + jnp.dot(ax[2], wx[ACROSS], preferred_element_type=jnp.float32)
     ).astype(jnp.bfloat16)
 
     w_share(ACROSS).wait_send()
     for side in (0, 1):
-        a_onward(side).wait_send()
+        for piece in (0, 1):
+            a_onward(side, piece).wait_send()
 
 
 def local(query_states, key_states, value_states, out_weight, block_docs):
@@ -328,8 +337,8 @@
             pltpu.SemaphoreType.DMA((COUNT,)),
             pltpu.SemaphoreType.DMA((9,)),
             pltpu.SemaphoreType.DMA((9,)),
-            pltpu.SemaphoreType.DMA((2, 3)),
-            pltpu.SemaphoreType.DMA((2, 3)),
+            pltpu.SemaphoreType.DMA((2, 6)),
+            pltpu.SemaphoreType.DMA((2, 6)),
         ],
         compiler_params=pltpu.CompilerParams(
             collective_id=0, has_side_effects=True, vmem_limit_bytes=20 << 20

time: 46.1 us -> 46.2 us (level)
  no operation moved by 1% of the time
where the time goes in v6:
time: 46.2 us; the launch traced here: 46.1 us
  Pallas kernels  45.4 us (98%)
  local copies, waits for them, and re-layouts  0.71 us (2%)
    pallas_call x1, Pallas kernels, local(): pl.pallas_call(kernel, out_shape=jax.ShapeDtypeStruct((tokens, width), jn...  45.4 us

profile of v6, /device:TPU:1, one launch (start us, length us, event | category | flops | bytes accessed | tf_op | source)
XLA Modules:
  0.0 46.1 jit_solution(10439909105825839171)
XLA Ops:
  0.0 45.4 %shard_map.55 = bf16[128,1024]{1,0:T(8,128)(2,1)S(1)} custom-call(s32[128]{0:T(128)} %docs_hbm.1, bf16[128,512]{1,0:T(8,128)(2,1)} %q_hbm.1, bf16[128,128]{1,0:T(8,128)(2,1)} %k_hbm.1, bf16[128,128]{1,0:T(8,128)(2,1)} %v_hbm.1, bf16[512,4096]{1,0:T(8,128)(2,1)} %w_hbm.1), custom_call_target="tpu_custom_call" | custom-call | tf_op jit(solution)/shard_map/pallas_call | solution.py:315
  45.4 0.7 %copy.7 = bf16[128,1024]{1,0:T(8,128)(2,1)} copy(bf16[128,1024]{1,0:T(8,128)(2,1)S(1)} %shard_map.55) | data formatting | bytes 524288
